TPU v7x, 32 devices: a whole 2x2x4 slice. The times are simulated.
32 devices in a mesh: group: 2 (over y), dp: 8 (over z, x), tensor: 2 (over core).
Axes of the slice: x: 2, y: 2, z: 4, core: 2. Of those that a mesh axis runs over, the one named last changes fastest.
Arguments:
- inputs: bfloat16 [12288, 1536], P(('group', 'dp')), may hold values from -6 to 6
- cotangent: bfloat16 [12288, 1536], P(('group', 'dp')), may hold values from -6 to 6
- lengths: int32 [16, 3], P(('group', 'dp')), may hold values from 1 to 576, 768 in all within a row
- attn_gain: bfloat16 [1536], P('dp'), may hold values from 0.25 to 1.75
- w_query: bfloat16 [1536, 1536], P('dp', 'tensor'), may hold values from -0.15625 to 0.15625
- b_query: bfloat16 [1536], P('tensor'), may hold values from -3 to 3
- w_key: bfloat16 [1536, 256], P('dp', 'tensor'), may hold values from -0.15625 to 0.15625
- b_key: bfloat16 [256], P('tensor'), may hold values from -3 to 3
- w_value: bfloat16 [1536, 256], P('dp', 'tensor'), may hold values from -0.15625 to 0.15625
- b_value: bfloat16 [256], P('tensor'), may hold values from -3 to 3
- w_out: bfloat16 [1536, 1536], P('dp', 'tensor'), may hold values from -1.25 to 1.25
- ffn_gain: bfloat16 [1536], P('dp'), may hold values from 0.25 to 1.75
- w_gate: bfloat16 [1536, 8960], P('dp', 'tensor'), may hold values from -0.15625 to 0.15625
- w_up: bfloat16 [1536, 8960], P('dp', 'tensor'), may hold values from -0.15625 to 0.15625
- w_down: bfloat16 [1536, 8960], P('dp', 'tensor'), may hold values from -0.0625 to 0.0625
Outputs:
- layer_out: bfloat16 [12288, 1536], P(('group', 'dp'))
- input_grad: bfloat16 [12288, 1536], P(('group', 'dp'))
- attn_gain_grad: float32 [1536], P('dp')
- w_query_grad: float32 [1536, 1536], P('dp', 'tensor')
- b_query_grad: float32 [1536], P('tensor')
- w_key_grad: float32 [1536, 256], P('dp', 'tensor')
- b_key_grad: float32 [256], P('tensor')
- w_value_grad: float32 [1536, 256], P('dp', 'tensor')
- b_value_grad: float32 [256], P('tensor')
- w_out_grad: float32 [1536, 1536], P('dp', 'tensor')
- ffn_gain_grad: float32 [1536], P('dp')
- w_gate_grad: float32 [1536, 8960], P('dp', 'tensor')
- w_up_grad: float32 [1536, 8960], P('dp', 'tensor')
- w_down_grad: float32 [1536, 8960], P('dp', 'tensor')
Inputs may be any that keep to these rules, and one draw needn't show every extreme that they name: In every stream the 3 lengths sum to 768, and the longest is exactly 576.
All inputs are finite; a program needn't handle non-finite values.
Results may differ from a plain program's by a relative error of at most 0.017.
Values may be sent and summed in bfloat16 or wider, within the bound.
No kernel may reach another device: no remote copies, remote signals or barrier semaphores. Data moves between devices by JAX's collectives and lax.ppermute only.
A program may use at most 384 MiB of HBM per device.

v0:
```python
import math

import jax
import jax.numpy as jnp
from jax import lax
from jax.sharding import PartitionSpec as P

HD = 128
SEQ = 768
NSEG = 3


EPSILON = 1e-06
THETA = 10000.0
MASKED_SCORE = -1e30


def normalize(values):
    return values * lax.rsqrt(jnp.mean(values * values, axis=-1, keepdims=True) + EPSILON)


def scaled_norm(values, gain_vec):
    return normalize(values) * gain_vec


def rotate(values, cosine, sine_table):
    half_width = values.shape[-1] // 2
    turned = jnp.concatenate([-values[..., half_width:], values[..., :half_width]], axis=-1)
    return values * cosine + turned * sine_table


def unrotate(values, cosine, sine_table):
    half_width = values.shape[-1] // 2
    sined = values * sine_table
    turned = jnp.concatenate([sined[..., half_width:], -sined[..., :half_width]], axis=-1)
    return values * cosine + turned


def layout(lengths):
    segment_ends = jnp.cumsum(lengths, axis=-1)
    segment_starts = segment_ends - lengths
    places = jnp.arange(SEQ, dtype=jnp.int32)
    segment = jnp.sum((places[:, None] >= segment_ends[..., None, :]).astype(jnp.int32), axis=-1)
    choose = segment[..., None] == jnp.arange(NSEG, dtype=jnp.int32)
    picked = jnp.sum(jnp.where(choose, segment_starts[..., None, :], 0), axis=-1)
    return (segment, places - picked)


def angles(position):
    frequency = jnp.exp(-(math.log(THETA) * 2.0 / HD) * jnp.arange(HD // 2, dtype=jnp.float32))
    phase_angle = position.astype(jnp.float32)[..., None] * frequency
    phase_angle = jnp.concatenate([phase_angle, phase_angle], axis=-1)
    return (jnp.cos(phase_angle), jnp.sin(phase_angle))


def plain_dot(left_side, right_side):
    return jnp.dot(left_side, right_side, preferred_element_type=jnp.float32)


def trans_dot(left_side, right_side):
    return lax.dot_general(
        left_side, right_side, (((1,), (1,)), ((), ())), preferred_element_type=jnp.float32
    )


def outer_dot(left_side, right_side):
    return lax.dot_general(
        left_side, right_side, (((0,), (0,)), ((), ())), preferred_element_type=jnp.float32
    )


def masked_scores(queries, keys_rot, allowed):
    raw_scores = jnp.einsum("qkgd,skd->kgqs", queries, keys_rot, preferred_element_type=jnp.float32)
    return jnp.where(allowed, raw_scores * HD ** (-0.5), MASKED_SCORE)


def local(
    inputs,
    cotangent,
    lengths,
    attn_gain,
    w_query,
    b_query,
    w_key,
    b_key,
    w_value,
    b_value,
    w_out,
    ffn_gain,
    w_gate,
    w_up,
    w_down,
):
    stream = inputs.astype(jnp.float32)
    segment, position = layout(lengths[0])
    cosine, sine_table = angles(position)
    cosine = cosine[:, None, :]
    sine_table = sine_table[:, None, :]
    places = jnp.arange(SEQ, dtype=jnp.int32)
    allowed = (segment[:, None] == segment[None, :]) & (places[None, :] <= places[:, None])
    score_scale = HD ** (-0.5)
    head_count = w_query.shape[1] // HD
    kv_count = w_key.shape[1] // HD
    group_size = head_count // kv_count
    d_model = inputs.shape[1]
    dp_count = lax.axis_size("dp")
    shard_rows = d_model // dp_count
    attn_set = (
        lax.all_gather(attn_gain, "dp", axis=0, tiled=True),
        lax.all_gather(w_query, "dp", axis=0, tiled=True),
        lax.all_gather(w_key, "dp", axis=0, tiled=True),
        lax.all_gather(w_value, "dp", axis=0, tiled=True),
        lax.all_gather(w_out, "dp", axis=0, tiled=True),
    )
    gain_one, query_full, key_full, value_full, out_full = attn_set
    gain_one_f = gain_one.astype(jnp.float32)
    h_one = scaled_norm(stream, gain_one_f).astype(jnp.bfloat16)
    query_pre = plain_dot(h_one, query_full) + b_query.astype(jnp.float32)
    key_pre = plain_dot(h_one, key_full) + b_key.astype(jnp.float32)
    value_pre = plain_dot(h_one, value_full) + b_value.astype(jnp.float32)
    queries = rotate(query_pre.reshape(SEQ, head_count, HD), cosine, sine_table).astype(
        jnp.bfloat16
    )
    queries = queries.reshape(SEQ, kv_count, group_size, HD)
    keys_rot = rotate(key_pre.reshape(SEQ, kv_count, HD), cosine, sine_table).astype(jnp.bfloat16)
    values_low = value_pre.astype(jnp.bfloat16).reshape(SEQ, kv_count, HD)
    scores = masked_scores(queries, keys_rot, allowed)
    row_max = jnp.max(scores, axis=-1, keepdims=True)
    exp_terms = jnp.exp(scores - row_max)
    row_total = jnp.sum(exp_terms, axis=-1, keepdims=True)
    log_total = row_max + jnp.log(row_total)
    probs_low = (exp_terms / row_total).astype(jnp.bfloat16)
    attended = jnp.einsum(
        "kgqs,skd->qkgd", probs_low, values_low, preferred_element_type=jnp.float32
    )
    attended = attended.reshape(SEQ, head_count * HD).astype(jnp.bfloat16)
    branch = lax.psum(trans_dot(attended, out_full), "tensor")
    residual = stream + branch
    ffn_set = (
        lax.all_gather(ffn_gain, "dp", axis=0, tiled=True),
        lax.all_gather(w_gate, "dp", axis=0, tiled=True),
        lax.all_gather(w_up, "dp", axis=0, tiled=True),
        lax.all_gather(w_down, "dp", axis=0, tiled=True),
    )
    gain_two, gate_full, up_full, down_full = ffn_set
    gain_two_f = gain_two.astype(jnp.float32)
    h_two = scaled_norm(residual, gain_two_f).astype(jnp.bfloat16)
    gate_pre = plain_dot(h_two, gate_full)
    up_pre = plain_dot(h_two, up_full)
    sigmoid_gate = jax.nn.sigmoid(gate_pre)
    swish_gate = gate_pre * sigmoid_gate
    hidden = (swish_gate * up_pre).astype(jnp.bfloat16)
    ffn_total = lax.psum(trans_dot(hidden, down_full).astype(jnp.bfloat16), "tensor").astype(
        jnp.float32
    )
    layer_out = (residual + ffn_total).astype(jnp.bfloat16)
    gain_two, gate_full, up_full, down_full = (
        lax.all_gather(ffn_gain, "dp", axis=0, tiled=True),
        lax.all_gather(w_gate, "dp", axis=0, tiled=True),
        lax.all_gather(w_up, "dp", axis=0, tiled=True),
        lax.all_gather(w_down, "dp", axis=0, tiled=True),
    )
    gain_two_f = gain_two.astype(jnp.float32)
    d_hidden = plain_dot(cotangent, down_full)
    d_gate = (d_hidden * up_pre * sigmoid_gate * (1.0 + gate_pre * (1.0 - sigmoid_gate))).astype(
        jnp.bfloat16
    )
    d_up = (d_hidden * swish_gate).astype(jnp.bfloat16)
    entry_two = trans_dot(d_gate, gate_full) + trans_dot(d_up, up_full)
    d_h_two = lax.psum(entry_two, "tensor")
    norm_two_back = jax.vjp(scaled_norm, residual, gain_two_f)[1]
    d_resid_norm, d_gain_two = norm_two_back(d_h_two)
    d_resid = cotangent.astype(jnp.float32) + d_resid_norm
    left_cols = h_two
    grad_cols = cotangent
    ffn_shard = lax.psum_scatter(
        jnp.concatenate(
            [
                outer_dot(left_cols, d_gate),
                outer_dot(left_cols, d_up),
                outer_dot(grad_cols, hidden),
            ],
            axis=1,
        ),
        "dp",
        scatter_dimension=0,
        tiled=True,
    )
    gain_one, query_full, key_full, value_full, out_full = (
        lax.all_gather(attn_gain, "dp", axis=0, tiled=True),
        lax.all_gather(w_query, "dp", axis=0, tiled=True),
        lax.all_gather(w_key, "dp", axis=0, tiled=True),
        lax.all_gather(w_value, "dp", axis=0, tiled=True),
        lax.all_gather(w_out, "dp", axis=0, tiled=True),
    )
    gain_one_f = gain_one.astype(jnp.float32)
    d_out_low = d_resid.astype(jnp.bfloat16)
    d_attended = (
        plain_dot(d_out_low, out_full).astype(jnp.bfloat16).reshape(SEQ, kv_count, group_size, HD)
    )
    scores = masked_scores(queries, keys_rot, allowed)
    probabilities = jnp.exp(scores - log_total)
    d_probs = jnp.einsum(
        "qkgd,skd->kgqs", d_attended, values_low, preferred_element_type=jnp.float32
    )
    d_value = jnp.einsum(
        "kgqs,qkgd->skd",
        probabilities.astype(jnp.bfloat16),
        d_attended,
        preferred_element_type=jnp.float32,
    )
    d_value = d_value.reshape(SEQ, kv_count * HD).astype(jnp.bfloat16)
    d_scores = probabilities * (d_probs - jnp.sum(probabilities * d_probs, axis=-1, keepdims=True))
    d_scores = d_scores.astype(jnp.bfloat16)
    d_query_rot = (
        jnp.einsum("kgqs,skd->qkgd", d_scores, keys_rot, preferred_element_type=jnp.float32)
        * score_scale
    )
    d_key_rot = (
        jnp.einsum("kgqs,qkgd->skd", d_scores, queries, preferred_element_type=jnp.float32)
        * score_scale
    )
    d_query = (
        unrotate(d_query_rot.reshape(SEQ, head_count, HD), cosine, sine_table)
        .astype(jnp.bfloat16)
        .reshape(SEQ, head_count * HD)
    )
    d_key = unrotate(d_key_rot, cosine, sine_table).astype(jnp.bfloat16).reshape(SEQ, kv_count * HD)
    entry_one = (
        trans_dot(d_query, query_full) + trans_dot(d_key, key_full) + trans_dot(d_value, value_full)
    )
    d_h_one = lax.psum(entry_one, "tensor")
    norm_one_back = jax.vjp(scaled_norm, stream, gain_one_f)[1]
    d_stream_norm, d_gain_one = norm_one_back(d_h_one)
    input_grad = (d_resid + d_stream_norm).astype(jnp.bfloat16)
    left_cols = h_one
    grad_cols = d_out_low
    attn_shard = lax.psum_scatter(
        jnp.concatenate(
            [
                outer_dot(left_cols, d_query),
                outer_dot(left_cols, d_key),
                outer_dot(left_cols, d_value),
                outer_dot(grad_cols, attended),
            ],
            axis=1,
        ),
        "dp",
        scatter_dimension=0,
        tiled=True,
    )
    attn_whole, ffn_whole = lax.psum((attn_shard, ffn_shard), "group")
    bias_query, bias_key, bias_value, gain_one_sum, gain_two_sum = lax.psum(
        (
            jnp.sum(d_query.astype(jnp.float32), axis=0),
            jnp.sum(d_key.astype(jnp.float32), axis=0),
            jnp.sum(d_value.astype(jnp.float32), axis=0),
            d_gain_one,
            d_gain_two,
        ),
        ("group", "dp"),
    )
    row_start = lax.axis_index("dp") * shard_rows
    gain_one_grad = lax.dynamic_slice_in_dim(gain_one_sum, row_start, shard_rows, 0)
    gain_two_grad = lax.dynamic_slice_in_dim(gain_two_sum, row_start, shard_rows, 0)
    query_cols = head_count * HD
    key_cols = kv_count * HD
    ffn_cols = w_gate.shape[1]
    query_grad = attn_whole[:, :query_cols]
    key_grad = attn_whole[:, query_cols : query_cols + key_cols]
    value_grad = attn_whole[:, query_cols + key_cols : query_cols + 2 * key_cols]
    out_grad = attn_whole[:, query_cols + 2 * key_cols :]
    gate_grad = ffn_whole[:, :ffn_cols]
    up_grad = ffn_whole[:, ffn_cols : 2 * ffn_cols]
    down_grad = ffn_whole[:, 2 * ffn_cols :]
    return (
        layer_out,
        input_grad,
        gain_one_grad,
        query_grad,
        bias_query,
        key_grad,
        bias_key,
        value_grad,
        bias_value,
        out_grad,
        gain_two_grad,
        gate_grad,
        up_grad,
        down_grad,
    )


def solution(mesh):
    in_specs = (
        P(("group", "dp"), None),
        P(("group", "dp"), None),
        P(("group", "dp"), None),
        P("dp"),
        P("dp", "tensor"),
        P("tensor"),
        P("dp", "tensor"),
        P("tensor"),
        P("dp", "tensor"),
        P("tensor"),
        P("dp", "tensor"),
        P("dp"),
        P("dp", "tensor"),
        P("dp", "tensor"),
        P("dp", "tensor"),
    )
    out_specs = (
        P(("group", "dp"), None),
        P(("group", "dp"), None),
        P("dp"),
        P("dp", "tensor"),
        P("tensor"),
        P("dp", "tensor"),
        P("tensor"),
        P("dp", "tensor"),
        P("tensor"),
        P("dp", "tensor"),
        P("dp"),
        P("dp", "tensor"),
        P("dp", "tensor"),
        P("dp", "tensor"),
    )
    return jax.shard_map(local, mesh=mesh, in_specs=in_specs, out_specs=out_specs, check_vma=False)
```

profile of v0, /device:TPU:0, one launch (start us, length us, event | category | flops | bytes accessed | tf_op | source)
XLA Modules:
  0.0 2713.8 jit_solution(7674493731302182500)
XLA Ops:
  20.0 23.5 all-reduce.4
  43.5 32.6 %all_gather.38 = bf16[1536,128]{1,0:T(8,128)(2,1)S(1)} all-gather(bf16[192,128]{1,0:T(8,128)(2,1)} %param.21), channel_id=1, replica_groups=mesh['group'=2,'dp'=8,'tensor'=2] {'dp'}, dimensions={0}, use_global_device_ids=true | all-gather | bytes 442368 | tf_op jit(solution)/shard_map/all_gather | solution.py:111
  76.1 32.4 %all_gather.37 = bf16[1536,128]{1,0:T(8,128)(2,1)S(1)} all-gather(bf16[192,128]{1,0:T(8,128)(2,1)} %param.23), channel_id=1, replica_groups=mesh['group'=2,'dp'=8,'tensor'=2] {'dp'}, dimensions={0}, use_global_device_ids=true | all-gather | bytes 442368 | tf_op jit(solution)/shard_map/all_gather | solution.py:112
  140.4 24.4 all-reduce.11.cloned.1.call-done
  170.5 188.1 %all-gather.12.cloned.1.call-done = bf16[1536,4480]{1,0:T(8,128)(2,1)} async-done(((bf16[192,4480]{1,0:T(8,128)(2,1)}), bf16[1536,4480]{1,0:T(8,128)(2,1)}) %all-gather.12.cloned.1.call-update) | async-done | bytes 13762576 | tf_op jit(solution)/shard_map/all_gather | solution.py:142
  358.6 17.1 fusion.78
  375.7 173.6 %all-gather.10.cloned.1.call-done = bf16[1536,4480]{1,0:T(8,128)(2,1)} async-done(((bf16[192,4480]{1,0:T(8,128)(2,1)}), bf16[1536,4480]{1,0:T(8,128)(2,1)}) %all-gather.10.cloned.1.call-update) | async-done | bytes 13762576 | tf_op jit(solution)/shard_map/all_gather | solution.py:141
  549.3 17.8 fusion.77
  567.1 172.9 %all-gather.14.cloned.1.call-done = bf16[1536,4480]{1,0:T(8,128)(2,1)} async-done(((bf16[192,4480]{1,0:T(8,128)(2,1)}), bf16[1536,4480]{1,0:T(8,128)(2,1)}) %all-gather.14.cloned.1.call-update) | async-done | bytes 13762576 | tf_op jit(solution)/shard_map/all_gather | solution.py:143
  740.0 27.2 %multiply_convert_fusion = (bf16[768,4480]{1,0:T(8,128)(2,1)}, bf16[768,4480]{1,0:T(8,128)(2,1)}, bf16[768,4480]{1,0:T(8,128)(2,1)}) fusion(f32[768,4480]{1,0:T(8,128)} %fusion.77, f32[768,4480]{1,0:T(8,128)} %fusion.78, bf16[768,1536]{1,0:T(8,128)(2,1)S(1)} %copy-done.19, bf16[1536,4480]{1,0:T(8,128)(2,1)} %all-gather.14.cloned.1.call-done), kind=kOutput, calls=%fused_computation.11 | convolution fusion | flops 10621255680 | bytes 64290816 | tf_op jit(solution)/shard_map/dot_general | solution.py:57
  767.2 17.3 fusion.79
  784.6 16.6 convolution_add_fusion
  801.2 17.0 convolution_convert_fusion
  833.9 20.4 all-reduce.13.cloned.1.call-done
  902.9 12.1 copy.79
  916.7 18.1 fusion.82
  934.9 17.8 fusion.81
  952.7 15.4 convolution_bitcast_fusion
  968.1 54.7 %pad_maximum_fusion = f32[1536,13440]{1,0:T(8,128)} fusion(f32[1536,4480]{1,0:T(8,128)} %convolution_bitcast_fusion, f32[1536,4480]{1,0:T(8,128)} %fusion.82, f32[1536,4480]{1,0:T(8,128)} %fusion.81), kind=kLoop, calls=%fused_computation | loop fusion | flops 41287680 | bytes 165150720 | tf_op jit(solution)/shard_map/concatenate | solution.py:177
  1030.7 71.2 %reduce-scatter.7.cloned.1.call-done = f32[192,1792]{1,0:T(8,128)} async-done(((f32[1536,1792]{1,0:T(8,128)}), f32[192,1792]{1,0:T(8,128)}) %reduce-scatter.7.cloned.1.call-update) | async-done | bytes 1376272
  1104.6 1272.6 %reduce-scatter.5.cloned.1.call-done = f32[192,13440]{1,0:T(8,128)} async-done(((f32[1536,13440]{1,0:T(8,128)}), f32[192,13440]{1,0:T(8,128)}) %reduce-scatter.5.cloned.1.call-update) | async-done | bytes 10321936 | tf_op jit(solution)/shard_map/reduce_scatter | solution.py:176
  2377.3 30.5 %all-reduce.17.cloned.1.call-done = f32[768,1536]{1,0:T(8,128)} async-done(((f32[768,1536]{1,0:T(8,128)}), f32[768,1536]{1,0:T(8,128)}) %all-reduce.17.cloned.1.call-update) | async-done | bytes 4718608 | tf_op jit(solution)/shard_map/psum | solution.py:232
  2411.6 78.4 %all-reduce.2 = (f32[1536]{0:T(1024)S(1)}, f32[768]{0:T(1024)}, f32[128]{0:T(128)}, f32[128]{0:T(128)}, f32[1536]{0:T(1024)S(1)}) all-reduce(f32[1536]{0:T(1024)S(1)} %get-tuple-element.58, f32[768]{0:T(1024)S(1)} %bitcast.185, f32[128]{0:T(128)S(1)} %get-tuple-element.69, ...), channel_id=1, replica_groups=mesh['group'=2,'dp'=8,'tensor'=2] {'group','dp'}, use_global_device_ids=true, to_apply=%region_15.16 | all-reduce | flops 4096 | bytes 32768 | tf_op jit(solution)/shard_map/psum | solution.py:253
  2496.8 195.3 %all-reduce.19.cloned.1.call-done = (f32[192,1792]{0,1:T(8,128)}, f32[192,13440]{1,0:T(8,128)}) async-done(((f32[192,1792]{0,1:T(8,128)}, f32[192,13440]{1,0:T(8,128)}), (f32[192,1792]{0,1:T(8,128)}, f32[192,13440]{1,0:T(8,128)})) %all-reduce.19.cloned.1.call-update) | async-done | bytes 11698192 | tf_op jit(solution)/shard_map/psum | solution.py:252
  (232 shorter events, 150.6 us)
Async XLA Ops:
  7.2 101.3 %copy-start.2 = (bf16[768,1536]{1,0:T(8,128)(2,1)S(1)}, bf16[768,1536]{1,0:T(8,128)(2,1)}, u32[]{:S(2)}) copy-start(bf16[768,1536]{1,0:T(8,128)(2,1)} %param.15) | copy-start | bytes 7077892
  7.2 106.2 %all-gather.6.cloned.1.call-start = ((), (), s32[]{:S(2)}) async-start(), calls=%async_computation.2 | async-start | bytes 2654208 | tf_op jit(solution)/shard_map/all_gather | solution.py:110
  7.9 124.1 %all-gather.8.cloned.1.call-start = ((), (), s32[]{:S(2)}) async-start(), calls=%async_computation.3 | async-start | bytes 2654208 | tf_op jit(solution)/shard_map/all_gather | solution.py:113
  8.7 156.1 %all-reduce.11.cloned.1.call-start = ((), (), s32[]{:S(2)}) async-start(), calls=%async_computation.4 | async-start | bytes 9437184 | tf_op jit(solution)/shard_map/psum | solution.py:137
  15.7 94.4 %copy-start.44 = (f32[768]{0:T(1024)}, f32[768]{0:T(1024)S(1)}, u32[]{:S(2)}) copy-start(f32[768]{0:T(1024)S(1)} %fusion.66) | copy-start | bytes 9220
  43.5 66.6 %copy-start.36 = (f32[1536]{0:T(1024)}, f32[1536]{0:T(1024)S(1)}, u32[]{:S(2)}) copy-start(f32[1536]{0:T(1024)S(1)} %convert_element_type.138) | copy-start | bytes 18436
  76.1 34.8 %copy-start.17 = (bf16[1536,128]{1,0:T(8,128)(2,1)}, bf16[1536,128]{1,0:T(8,128)(2,1)S(1)}, u32[]{:S(2)}) copy-start(bf16[1536,128]{1,0:T(8,128)(2,1)S(1)} %all_gather.38) | copy-start | bytes 1179652
  138.4 220.2 %all-gather.12.cloned.1.call-start = ((), (), s32[]{:S(2)}) async-start(), calls=%async_computation.6 | async-start | bytes 15482880 | tf_op jit(solution)/shard_map/all_gather | solution.py:142
  139.0 410.3 %all-gather.10.cloned.1.call-start = ((), (), s32[]{:S(2)}) async-start(), calls=%async_computation.5 | async-start | bytes 15482880 | tf_op jit(solution)/shard_map/all_gather | solution.py:141
  139.6 600.5 %all-gather.14.cloned.1.call-start = ((), (), s32[]{:S(2)}) async-start(), calls=%async_computation.7 | async-start | bytes 15482880 | tf_op jit(solution)/shard_map/all_gather | solution.py:143
  140.1 688.3 %all-reduce.15.cloned.1.call-start = ((), (), s32[]{:S(2)}) async-start(), calls=%async_computation.9 | async-start | bytes 9437184 | tf_op jit(solution)/shard_map/psum | solution.py:170
  170.5 188.1 %copy-start.21 = (bf16[768,1536]{1,0:T(8,128)(2,1)}, bf16[768,1536]{1,0:T(8,128)(2,1)S(1)}, u32[]{:S(2)}) copy-start(bf16[768,1536]{1,0:T(8,128)(2,1)S(1)} %multiply_convert_fusion.3) | copy-start | bytes 7077892
  375.7 364.4 %copy-start.19 = (bf16[768,1536]{1,0:T(8,128)(2,1)S(1)}, bf16[768,1536]{1,0:T(8,128)(2,1)}, u32[]{:S(2)}) copy-start(bf16[768,1536]{1,0:T(8,128)(2,1)} %param.16) | copy-start | bytes 7077892
  801.1 53.1 %all-reduce.13.cloned.1.call-start = ((), (), s32[]{:S(2)}) async-start(), calls=%async_computation.8 | async-start | bytes 4718592 | tf_op jit(solution)/shard_map/psum | solution.py:153
  818.2 283.7 %reduce-scatter.7.cloned.1.call-start = ((), (), s32[]{:S(2)}) async-start(), calls=%async_computation.12 | async-start | bytes 12386304
  915.1 1462.1 %reduce-scatter.5.cloned.1.call-start = ((), (), s32[]{:S(2)}) async-start(), calls=%async_computation.11 | async-start | bytes 92897280 | tf_op jit(solution)/shard_map/reduce_scatter | solution.py:176
  916.7 35.9 %slice-start.6 = ((s8[6881280]{0:T(1024)(128)(4,1)}), s8[4194304]{0:T(1024)(128)(4,1)S(1)}, s32[]{:S(2)}) async-start(s8[6881280]{0:T(1024)(128)(4,1)} %bitcast.190), calls=%async_computation.20 | async-start | bytes 8388608
  1022.8 1385.0 %all-reduce.17.cloned.1.call-start = ((), (), s32[]{:S(2)}) async-start(), calls=%async_computation.10 | async-start | bytes 9437184 | tf_op jit(solution)/shard_map/psum | solution.py:232
  1030.7 1661.4 %all-reduce.19.cloned.1.call-start = ((), (), s32[]{:S(2)}) async-start(), calls=%async_computation.13 | async-start | bytes 24313856 | tf_op jit(solution)/shard_map/psum | solution.py:252
  2377.2 30.5 %copy-start.45 = (f32[768]{0:T(1024)S(1)}, f32[768]{0:T(1024)}, u32[]{:S(2)}) copy-start(f32[768]{0:T(1024)} %copy-done.44) | copy-start | bytes 9220
  2377.3 34.3 %copy-start.50 = (f32[1536]{0:T(1024)S(1)}, f32[1536]{0:T(1024)}, u32[]{:S(2)}) copy-start(f32[1536]{0:T(1024)} %get-tuple-element.56) | copy-start | bytes 18436
  2377.3 34.3 %copy-start.51 = (f32[6,128]{1,0:T(8,128)S(1)}, f32[6,128]{1,0:T(8,128)}, u32[]{:S(2)}) copy-start(f32[6,128]{1,0:T(8,128)} %get-tuple-element.81) | copy-start | bytes 9220
  2377.3 34.3 %copy-start.52 = (f32[128]{0:T(128)S(1)}, f32[128]{0:T(128)}, u32[]{:S(2)}) copy-start(f32[128]{0:T(128)} %get-tuple-element.108) | copy-start | bytes 1540
  2377.3 114.0 %copy-start.47 = (f32[768]{0:T(1024)S(1)}, f32[768]{0:T(1024)}, u32[]{:S(2)}) copy-start(f32[768]{0:T(1024)} %copy-done.46) | copy-start | bytes 9220
  (53 other events, 428.7 us)
Sparse Core Ops, SparseCore 0:
  10.2 60.1 all-gather.5
  72.5 51.7 all-gather.7
  138.5 26.2 all-reduce.10
  166.9 191.6 all-gather.11
  360.6 188.6 all-gather.9
  551.3 188.6 all-gather.13
  801.3 27.0 all-reduce.14
  831.3 22.9 all-reduce.12
  915.2 186.6 reduce-scatter.6
  1105.7 1271.4 reduce-scatter.4
  2379.7 27.9 all-reduce.16
  2410.7 281.3 all-reduce.18
where the time goes:
time: 2720 us; the launch traced here: 2710 us
  waiting for transfers between devices  2160 us (79%)
  matrix products  213 us (8%)
  blocking collectives  167 us (6%)
  other arithmetic  107 us (4%)
  local copies, waits for them, and re-layouts  48 us (2%)
    reduce_scatter x1, waiting for transfers between devices, local(): lax.psum_scatter(jnp.concatenate([outer_dot(left_cols, d_gate), outer_dot...  1270 us
    psum x1, waiting for transfers between devices, local(): attn_whole, ffn_whole = lax.psum((attn_shard, ffn_shard), 'group')  195 us
    all_gather x1, waiting for transfers between devices, local(): lax.all_gather(w_up, 'dp', axis=0, tiled=True)  188 us
    all_gather x1, waiting for transfers between devices, local(): lax.all_gather(w_gate, 'dp', axis=0, tiled=True)  174 us
    all_gather x1, waiting for transfers between devices, local(): lax.all_gather(w_down, 'dp', axis=0, tiled=True)  173 us
    psum x1, blocking collectives, local(): lax.psum((jnp.sum(d_query.astype(jnp.float32), axis=0), jnp.sum(d_key.ast...  78.4 us
    unnamed x13, waiting for transfers between devices  74.3 us
    dot_general x7, matrix products, plain_dot(): return jnp.dot(left_side, right_side, preferred_element_type=jnp.float32)  70.7 us
  transfers between devices with their start and end apart: 12, of which 10 were waited for; matrix products, arithmetic and copies ran while one was open for 8% of the time, Pallas kernels for 0%

commit v1 on v0

v1 whole, which is shorter than its diff:
```python
import math

import jax
import jax.numpy as jnp
from jax import lax
from jax.sharding import PartitionSpec as P

HD = 128
SEQ = 768
NSEG = 3


EPSILON = 1e-06
THETA = 10000.0
MASKED_SCORE = -1e30


def normalize(values):
    return values * lax.rsqrt(jnp.mean(values * values, axis=-1, keepdims=True) + EPSILON)


def scaled_norm(values, gain_vec):
    return normalize(values) * gain_vec


def rotate(values, cosine, sine_table):
    half_width = values.shape[-1] // 2
    turned = jnp.concatenate([-values[..., half_width:], values[..., :half_width]], axis=-1)
    return values * cosine + turned * sine_table


def unrotate(values, cosine, sine_table):
    half_width = values.shape[-1] // 2
    sined = values * sine_table
    turned = jnp.concatenate([sined[..., half_width:], -sined[..., :half_width]], axis=-1)
    return values * cosine + turned


def layout(lengths):
    segment_ends = jnp.cumsum(lengths, axis=-1)
    segment_starts = segment_ends - lengths
    places = jnp.arange(SEQ, dtype=jnp.int32)
    segment = jnp.sum((places[:, None] >= segment_ends[..., None, :]).astype(jnp.int32), axis=-1)
    choose = segment[..., None] == jnp.arange(NSEG, dtype=jnp.int32)
    picked = jnp.sum(jnp.where(choose, segment_starts[..., None, :], 0), axis=-1)
    return (segment, places - picked)


def angles(position):
    frequency = jnp.exp(-(math.log(THETA) * 2.0 / HD) * jnp.arange(HD // 2, dtype=jnp.float32))
    phase_angle = position.astype(jnp.float32)[..., None] * frequency
    phase_angle = jnp.concatenate([phase_angle, phase_angle], axis=-1)
    return (jnp.cos(phase_angle), jnp.sin(phase_angle))


def plain_dot(left_side, right_side):
    return jnp.dot(left_side, right_side, preferred_element_type=jnp.float32)


def trans_dot(left_side, right_side):
    return lax.dot_general(
        left_side, right_side, (((1,), (1,)), ((), ())), preferred_element_type=jnp.float32
    )


def outer_dot(left_side, right_side):
    return lax.dot_general(
        left_side, right_side, (((0,), (0,)), ((), ())), preferred_element_type=jnp.float32
    )


def masked_scores(queries, keys_rot, allowed):
    raw_scores = jnp.einsum("qkgd,skd->kgqs", queries, keys_rot, preferred_element_type=jnp.float32)
    return jnp.where(allowed, raw_scores * HD ** (-0.5), MASKED_SCORE)


AXES = ("group", "dp", "tensor")


def routes(dp_count):
    def table(move):
        flat = lambda g, d, t: (g * dp_count + d) * 2 + t
        return [
            (flat(g, d, t), flat(*move(g, d, t)))
            for g in range(2)
            for d in range(dp_count)
            for t in range(2)
        ]

    return {
        "x": table(lambda g, d, t: (g, d ^ 1, t)),
        "y": table(lambda g, d, t: (g ^ 1, d, t)),
        "t": table(lambda g, d, t: (g, d, t ^ 1)),
        "first": table(lambda g, d, t: (g, d ^ 1, t) if t == 0 else (g ^ 1, d, t)),
        "second": table(lambda g, d, t: (g ^ 1, d, t) if t == 0 else (g, d ^ 1, t)),
    }


def local(
    inputs,
    cotangent,
    lengths,
    attn_gain,
    w_query,
    b_query,
    w_key,
    b_key,
    w_value,
    b_value,
    w_out,
    ffn_gain,
    w_gate,
    w_up,
    w_down,
):
    bf16 = jnp.bfloat16
    f32 = jnp.float32
    dp_count = lax.axis_size("dp")
    line = dp_count // 2
    dp_index = lax.axis_index("dp")
    x_index = dp_index % 2
    y_index = lax.axis_index("group")
    core = lax.axis_index("tensor")
    table = routes(dp_count)
    line_groups = [[2 * z + x for z in range(line)] for x in range(2)]
    tokens, d_model = inputs.shape
    half = tokens // 2
    rows = w_query.shape[0]
    head_count = w_query.shape[1] // HD
    kv_count = w_key.shape[1] // HD
    group_size = head_count // kv_count
    ffn_cols = w_gate.shape[1]
    quarter = -(-ffn_cols // 512) * 128
    score_scale = HD ** (-0.5)

    def send(value, route):
        return lax.ppermute(value, AXES, table[route])

    def pick(value, index):
        return lax.dynamic_index_in_dim(value, index, 0, keepdims=False)

    def in_order(index, mine, other):
        first = index == 0
        return jnp.where(first, mine, other), jnp.where(first, other, mine)

    def my_half(value):
        return pick(value.reshape(2, half, value.shape[-1]), core)

    def other_half(value):
        return pick(value.reshape(2, half, value.shape[-1]), 1 - core)

    def both_halves(mine):
        return jnp.concatenate(in_order(core, mine, send(mine, "t")), axis=0)

    def square_gather(mine):
        near = send(mine, "first")
        mine_sib = send(mine, "t")
        far = send(jnp.stack([mine, near]), "second")
        near_sib = send(near, "t")
        far_sib = send(far, "t")
        return jnp.concatenate(
            [mine, near, far[0], far[1], mine_sib, near_sib, far_sib[0], far_sib[1]], axis=0
        )

    def square_scatter(mine, theirs):
        came = send(theirs.astype(bf16), "t")
        total = (mine.astype(f32) + came.astype(f32)).reshape(4, half, d_model)
        came = send(total[2:].astype(bf16), "second")
        total = total[:2] + came.astype(f32)
        came = send(total[1].astype(bf16), "first")
        return total[0] + came.astype(f32)

    def ffn_gather(weight):
        padded = jnp.pad(weight, ((0, 0), (0, 4 * quarter - ffn_cols)))
        parts = padded.reshape(rows, 4, quarter).transpose(1, 0, 2)
        mine = pick(parts, x_index * 2 + y_index)
        came = send(pick(parts, (1 - x_index) * 2 + y_index), "x")
        pair = jnp.stack(in_order(x_index, mine, came))
        full = lax.all_gather(pair, "dp", axis=0, axis_index_groups=line_groups)
        return full.reshape(d_model, quarter)

    def ffn_scatter(grad):
        parts = grad.astype(bf16).reshape(line, 2 * rows, quarter)
        summed = lax.psum_scatter(
            parts, "dp", scatter_dimension=0, axis_index_groups=line_groups
        ).reshape(2, rows, quarter)
        came = send(pick(summed, 1 - x_index), "x")
        pair = jnp.stack(in_order(x_index, pick(summed, x_index), came))
        low, high = in_order(y_index, pair, send(pair, "y"))
        whole = jnp.concatenate([low[0], high[0], low[1], high[1]], axis=1)
        return whole[:, :ffn_cols].astype(f32)

    def attn_scatter(grad):
        summed = lax.psum_scatter(
            grad.astype(bf16), "dp", scatter_dimension=0, tiled=True
        )
        return summed.astype(f32) + send(summed, "y").astype(f32)

    stream = inputs.astype(f32)
    segment, position = layout(lengths[0])
    cosine, sine_table = angles(position)
    cosine = cosine[:, None, :]
    sine_table = sine_table[:, None, :]
    places = jnp.arange(SEQ, dtype=jnp.int32)
    allowed = (segment[:, None] == segment[None, :]) & (places[None, :] <= places[:, None])

    gains = jnp.pad(
        jnp.stack([attn_gain, ffn_gain], axis=1), ((0, 0), (0, 126))
    )
    query_cols = head_count * HD
    key_cols = kv_count * HD
    qkv_cols = query_cols + 2 * key_cols
    qkv_full = lax.all_gather(
        jnp.concatenate([w_query, w_key, w_value, gains], axis=1), "dp", axis=0, tiled=True
    )
    out_full = lax.all_gather(w_out, "dp", axis=0, tiled=True)
    gate_full = ffn_gather(w_gate)
    up_full = ffn_gather(w_up)
    down_full = ffn_gather(w_down)
    cot_half = my_half(cotangent)
    cot_all = square_gather(cot_half)

    gain_one = qkv_full[:, qkv_cols].astype(f32)
    gain_two = qkv_full[:, qkv_cols + 1].astype(f32)
    qkv_full = qkv_full[:, :qkv_cols]

    inv_one = lax.rsqrt(jnp.mean(stream * stream, axis=-1, keepdims=True) + EPSILON)
    h_one = (stream * inv_one * gain_one).astype(bf16)
    qkv_bias = jnp.concatenate([b_query, b_key, b_value]).astype(f32)
    qkv_pre = plain_dot(h_one, qkv_full) + qkv_bias
    query_pre = qkv_pre[:, :query_cols]
    key_pre = qkv_pre[:, query_cols : query_cols + key_cols]
    value_pre = qkv_pre[:, query_cols + key_cols :]
    queries = rotate(query_pre.reshape(SEQ, head_count, HD), cosine, sine_table).astype(bf16)
    queries = queries.reshape(SEQ, kv_count, group_size, HD)
    keys_rot = rotate(key_pre.reshape(SEQ, kv_count, HD), cosine, sine_table).astype(bf16)
    values_low = value_pre.astype(bf16).reshape(SEQ, kv_count, HD)
    scores = masked_scores(queries, keys_rot, allowed)
    row_max = jnp.max(scores, axis=-1, keepdims=True)
    exp_terms = jnp.exp(scores - row_max)
    row_total = jnp.sum(exp_terms, axis=-1, keepdims=True)
    log_total = row_max + jnp.log(row_total)
    probs_low = (exp_terms / row_total).astype(bf16)
    attended = jnp.einsum("kgqs,skd->qkgd", probs_low, values_low, preferred_element_type=f32)
    attended = attended.reshape(SEQ, head_count * HD).astype(bf16)
    branch = trans_dot(attended, out_full)
    resid = (
        my_half(stream)
        + my_half(branch)
        + send(other_half(branch).astype(bf16), "t").astype(f32)
    )
    inv_two = lax.rsqrt(jnp.mean(resid * resid, axis=-1, keepdims=True) + EPSILON)
    norm_two = resid * inv_two
    h_two = square_gather((norm_two * gain_two).astype(bf16))

    gate_pre = plain_dot(h_two, gate_full)
    up_pre = plain_dot(h_two, up_full)
    sigmoid_gate = jax.nn.sigmoid(gate_pre)
    swish_gate = gate_pre * sigmoid_gate
    hidden = (swish_gate * up_pre).astype(bf16)
    down_grad = ffn_scatter(outer_dot(cot_all, hidden))
    d_hidden = plain_dot(cot_all, down_full)
    d_gate = (d_hidden * up_pre * sigmoid_gate * (1.0 + gate_pre * (1.0 - sigmoid_gate))).astype(
        bf16
    )
    d_up = (d_hidden * swish_gate).astype(bf16)
    mid = 4 * half

    def entry(part):
        return trans_dot(d_gate[part], gate_full) + trans_dot(d_up[part], up_full)

    d_h_two = square_scatter(entry(slice(0, mid)), entry(slice(mid, None)))
    gate_grad = ffn_scatter(outer_dot(h_two, d_gate))
    up_grad = ffn_scatter(outer_dot(h_two, d_up))
    ffn_total = square_scatter(
        trans_dot(hidden[:mid], down_full), trans_dot(hidden[mid:], down_full)
    )
    layer_out = both_halves((resid + ffn_total).astype(bf16))

    scaled = d_h_two * gain_two
    d_resid = cot_half.astype(f32) + inv_two * (
        scaled - norm_two * jnp.mean(norm_two * scaled, axis=-1, keepdims=True)
    )
    gain_two_part = jnp.sum(d_h_two * norm_two, axis=0)
    d_out_low = both_halves(d_resid.astype(bf16))
    out_grad = attn_scatter(outer_dot(d_out_low, attended))
    d_attended = (
        plain_dot(d_out_low, out_full).astype(bf16).reshape(SEQ, kv_count, group_size, HD)
    )
    scores = masked_scores(queries, keys_rot, allowed)
    probabilities = jnp.exp(scores - log_total)
    d_probs = jnp.einsum("qkgd,skd->kgqs", d_attended, values_low, preferred_element_type=f32)
    d_value = jnp.einsum(
        "kgqs,qkgd->skd", probabilities.astype(bf16), d_attended, preferred_element_type=f32
    )
    d_value = d_value.reshape(SEQ, kv_count * HD).astype(bf16)
    d_scores = probabilities * (d_probs - jnp.sum(probabilities * d_probs, axis=-1, keepdims=True))
    d_scores = d_scores.astype(bf16)
    d_query_rot = (
        jnp.einsum("kgqs,skd->qkgd", d_scores, keys_rot, preferred_element_type=f32) * score_scale
    )
    d_key_rot = (
        jnp.einsum("kgqs,qkgd->skd", d_scores, queries, preferred_element_type=f32) * score_scale
    )
    d_query = (
        unrotate(d_query_rot.reshape(SEQ, head_count, HD), cosine, sine_table)
        .astype(bf16)
        .reshape(SEQ, head_count * HD)
    )
    d_key = unrotate(d_key_rot, cosine, sine_table).astype(bf16).reshape(SEQ, kv_count * HD)
    d_qkv = jnp.concatenate([d_query, d_key, d_value], axis=1)
    qkv_grad = attn_scatter(outer_dot(h_one, d_qkv))
    entry_one = trans_dot(d_qkv, qkv_full)
    d_h_one = my_half(entry_one) + send(other_half(entry_one).astype(bf16), "t").astype(f32)
    half_inv = my_half(inv_one)
    norm_one = my_half(stream) * half_inv
    scaled = d_h_one * gain_one
    input_grad = both_halves(
        (
            d_resid
            + half_inv * (scaled - norm_one * jnp.mean(norm_one * scaled, axis=-1, keepdims=True))
        ).astype(bf16)
    )
    gain_one_part = jnp.sum(d_h_one * norm_one, axis=0)

    bias_part = jnp.sum(d_qkv.astype(f32), axis=0)
    small = jnp.concatenate([gain_one_part, gain_two_part, bias_part]).reshape(-1, 128)
    small = small + send(small, "y")
    step = 1
    while step < dp_count:
        small = small + lax.ppermute(small, "dp", [(i, i ^ step) for i in range(dp_count)])
        step *= 2
    small = small.reshape(-1)
    gain_sums = small[: 2 * d_model].reshape(2, dp_count, rows)
    mine = lax.dynamic_index_in_dim(gain_sums, dp_index, 1, keepdims=False)
    mine = mine + send(mine, "t")
    bias_sum = small[2 * d_model :]
    return (
        layer_out,
        input_grad,
        mine[0],
        qkv_grad[:, :query_cols],
        bias_sum[:query_cols],
        qkv_grad[:, query_cols : query_cols + key_cols],
        bias_sum[query_cols : query_cols + key_cols],
        qkv_grad[:, query_cols + key_cols :],
        bias_sum[query_cols + key_cols :],
        out_grad,
        mine[1],
        gate_grad,
        up_grad,
        down_grad,
    )


def solution(mesh):
    in_specs = (
        P(("group", "dp"), None),
        P(("group", "dp"), None),
        P(("group", "dp"), None),
        P("dp"),
        P("dp", "tensor"),
        P("tensor"),
        P("dp", "tensor"),
        P("tensor"),
        P("dp", "tensor"),
        P("tensor"),
        P("dp", "tensor"),
        P("dp"),
        P("dp", "tensor"),
        P("dp", "tensor"),
        P("dp", "tensor"),
    )
    out_specs = (
        P(("group", "dp"), None),
        P(("group", "dp"), None),
        P("dp"),
        P("dp", "tensor"),
        P("tensor"),
        P("dp", "tensor"),
        P("tensor"),
        P("dp", "tensor"),
        P("tensor"),
        P("dp", "tensor"),
        P("dp"),
        P("dp", "tensor"),
        P("dp", "tensor"),
        P("dp", "tensor"),
    )
    return jax.shard_map(local, mesh=mesh, in_specs=in_specs, out_specs=out_specs, check_vma=False)
```

time: 2720 us -> 877 us (0.32)
  waiting for transfers between devices: 2160 us -> 384 us
  blocking collectives: 167 us -> 0 us
  starting transfers between devices: 0.98 us -> 76.5 us
  other arithmetic: 107 us -> 66.3 us
  local copies, waits for them, and re-layouts: 48 us -> 87.7 us
    reduce_scatter x1 -> x5, waiting for transfers between devices: 1270 us -> 155 us  [the longest x3 88.7 us: ffn_scatter(): lax.psum_scatter(parts, 'dp', scatter_dimension=0, axis_index_groups=line...]
    all_gather x5, waiting for transfers between devices: 535 us -> 110 us  [the longest x3 77.1 us: ffn_gather(): full = lax.all_gather(pair, 'dp', axis=0, axis_index_groups=line_groups)]
    psum x5 -> x0, waiting for transfers between devices: 281 us -> none  [the longest x1 195 us: local(): attn_whole, ffn_whole = lax.psum((attn_shard, ffn_shard), 'group')]
    ppermute x0 -> x37, waiting for transfers between devices: none -> 118 us  [the longest x34 114 us: send(): return lax.ppermute(value, AXES, table[route])]
    psum x1 -> x0, blocking collectives: 78.4 us -> none  [local(): lax.psum((jnp.sum(d_query.astype(jnp.float32), axis=0), jnp.sum(d_key.ast...]
    ppermute x0 -> x37, starting transfers between devices: none -> 75.9 us  [the longest x34 70.9 us: send(): return lax.ppermute(value, AXES, table[route])]
    unnamed x13 -> x10, waiting for transfers between devices: 74.3 us -> 0.84 us
    all_gather x2 -> x0, blocking collectives: 65 us -> none  [the longest x1 32.6 us: local(): lax.all_gather(w_key, 'dp', axis=0, tiled=True)]
  transfers between devices with their start and end apart: 12 -> 47, of which waited for: 10 -> 21; matrix products, arithmetic and copies ran while one was open for 8% -> 38% of each run, Pallas kernels for 0% -> 0%
where the time goes in v1:
time: 877 us; the launch traced here: 870 us
  waiting for transfers between devices  384 us (44%)
  matrix products  240 us (27%)
  local copies, waits for them, and re-layouts  87.7 us (10%)
  starting transfers between devices  76.5 us (9%)
  other arithmetic  66.3 us (8%)
  between operations  15.9 us (2%)
    ppermute x34, waiting for transfers between devices, send(): return lax.ppermute(value, AXES, table[route])  114 us
    reduce_scatter x3, waiting for transfers between devices, ffn_scatter(): lax.psum_scatter(parts, 'dp', scatter_dimension=0, axis_index_groups=line...  88.7 us
    all_gather x3, waiting for transfers between devices, ffn_gather(): full = lax.all_gather(pair, 'dp', axis=0, axis_index_groups=line_groups)  77.1 us
    dot_general x8, matrix products, trans_dot(): lax.dot_general(left_side, right_side, (((1,), (1,)), ((), ())), preferre...  75.4 us
    dot_general x5, matrix products, plain_dot(): return jnp.dot(left_side, right_side, preferred_element_type=jnp.float32)  74.3 us
    ppermute x34, starting transfers between devices, send(): return lax.ppermute(value, AXES, table[route])  70.9 us
    reduce_scatter x2, waiting for transfers between devices, attn_scatter(): lax.psum_scatter(grad.astype(bf16), 'dp', scatter_dimension=0, tiled=True)  66.6 us
    dot_general x5, matrix products, outer_dot(): lax.dot_general(left_side, right_side, (((0,), (0,)), ((), ())), preferre...  59.6 us
  transfers between devices with their start and end apart: 47, of which 21 were waited for; matrix products, arithmetic and copies ran while one was open for 38% of the time, Pallas kernels for 0%

profile of v1, /device:TPU:0, one launch (start us, length us, event | category | flops | bytes accessed | tf_op | source)
XLA Modules:
  0.0 870.4 jit_solution(2815979763971457537)
XLA Ops:
  26.7 11.8 %collective-permute-done.7 = bf16[192,1152]{1,0:T(8,128)(2,1)S(1)} collective-permute-done((bf16[192,1152]{1,0:T(8,128)(2,1)S(1)}, bf16[192,1152]{1,0:T(8,128)(2,1)S(1)}, u32[]{:S(2)}, u32[]{:S(2)}) %collective-permute-start.7) | collective-permute-done | bytes 442400 | tf_op jit(solution)/shard_map/ppermute | solution.py:137
  52.6 14.3 %collective-permute-done.6 = bf16[192,1152]{1,0:T(8,128)(2,1)} collective-permute-done((bf16[192,1152]{1,0:T(8,128)(2,1)}, bf16[192,1152]{1,0:T(8,128)(2,1)}, u32[]{:S(2)}, u32[]{:S(2)}) %collective-permute-start.6) | collective-permute-done | bytes 442400 | tf_op jit(solution)/shard_map/ppermute | solution.py:137
  69.3 22.2 %all-gather.9.cloned.1.call-done = bf16[1536,1152]{1,0:T(8,128)(2,1)} async-done(((bf16[192,1152]{1,0:T(8,128)(2,1)}), bf16[1536,1152]{1,0:T(8,128)(2,1)}) %all-gather.9.cloned.1.call-update) | async-done | bytes 3538960 | tf_op jit(solution)/shard_map/all_gather | solution.py:213
  165.2 26.8 %collective-permute-done.14 = bf16[2,384,1536]{2,1,0:T(8,128)(2,1)} collective-permute-done((bf16[2,384,1536]{2,1,0:T(8,128)(2,1)S(1)}, bf16[2,384,1536]{2,1,0:T(8,128)(2,1)}, u32[]{:S(2)}, u32[]{:S(2)}) %collective-permute-start.14) | collective-permute-done | bytes 2359328 | tf_op jit(solution)/shard_map/ppermute | solution.py:137
  215.9 15.6 %collective-permute-done.2 = bf16[2,384,1536]{2,1,0:T(8,128)(2,1)S(1)} collective-permute-done((bf16[2,384,1536]{2,1,0:T(8,128)(2,1)S(1)}, bf16[2,384,1536]{2,1,0:T(8,128)(2,1)S(1)}, u32[]{:S(2)}, u32[]{:S(2)}) %collective-permute-start.2) | collective-permute-done | bytes 2359328 | tf_op jit(solution)/shard_map/ppermute | solution.py:137
  242.7 17.9 %fusion.106 = f32[3072,1152]{1,0:T(8,128)} fusion(bf16[3072,1536]{1,0:T(8,128)(2,1)} %fusion.60, bf16[1536,1152]{1,0:T(8,128)(2,1)} %bitcast.411), kind=kOutput, calls=%fused_computation.271 | convolution fusion | flops 10871635968 | bytes 27131904 | tf_op jit(solution)/shard_map/dot_general | solution.py:57
  260.6 24.4 %all-gather.13.cloned.1.call-done = bf16[8,192,1152]{2,1,0:T(8,128)(2,1)} async-done(((bf16[2,192,1152]{2,1,0:T(8,128)(2,1)}), bf16[8,192,1152]{2,1,0:T(8,128)(2,1)}) %all-gather.13.cloned.1.call-update) | async-done | bytes 3538960 | tf_op jit(solution)/shard_map/all_gather | solution.py:179
  285.0 17.9 %fusion.105 = f32[3072,1152]{1,0:T(8,128)} fusion(bf16[3072,1536]{1,0:T(8,128)(2,1)} %fusion.60, bf16[1536,1152]{1,0:T(8,128)(2,1)} %bitcast.414), kind=kOutput, calls=%fused_computation.270 | convolution fusion | flops 10871635968 | bytes 27131904 | tf_op jit(solution)/shard_map/dot_general | solution.py:57
  302.9 52.7 %all-gather.17.cloned.1.call-done = bf16[8,192,1152]{2,1,0:T(8,128)(2,1)} async-done(((bf16[2,192,1152]{2,1,0:T(8,128)(2,1)}), bf16[8,192,1152]{2,1,0:T(8,128)(2,1)}) %all-gather.17.cloned.1.call-update) | async-done | bytes 3538960 | tf_op jit(solution)/shard_map/all_gather | solution.py:179
  355.6 29.6 %multiply_convert_fusion = (bf16[3072,1152]{1,0:T(8,128)(2,1)}, bf16[3072,1152]{1,0:T(8,128)(2,1)}, bf16[3072,1152]{1,0:T(8,128)(2,1)}) fusion(f32[3072,1152]{1,0:T(8,128)} %fusion.105, f32[3072,1152]{1,0:T(8,128)} %fusion.106, bf16[3072,1536]{1,0:T(8,128)(2,1)} %fusion.56, bf16[1536,1152]{1,0:T(8,128)(2,1)} %bitcast.417), kind=kOutput, calls=%fused_computation.7 | convolution fusion | flops 10924720128 | bytes 62521344 | tf_op jit(solution)/shard_map/dot_general | solution.py:57
  385.2 18.1 %convolution_convert_fusion.1 = bf16[1536,1152]{1,0:T(8,128)(2,1)} fusion(bf16[3072,1536]{1,0:T(8,128)(2,1)} %fusion.56, bf16[3072,1152]{1,0:T(8,128)(2,1)} %get-tuple-element.30), kind=kOutput, calls=%fused_computation.20 | convolution fusion | flops 10873405440 | bytes 20054016 | tf_op jit(solution)/shard_map/dot_general | solution.py:67
  403.3 18.0 %convolution_convert_fusion.2 = bf16[1536,1152]{1,0:T(8,128)(2,1)} fusion(bf16[3072,1536]{1,0:T(8,128)(2,1)} %fusion.60, bf16[3072,1152]{1,0:T(8,128)(2,1)} %get-tuple-element.28), kind=kOutput, calls=%fused_computation.21 | convolution fusion | flops 10873405440 | bytes 20054016 | tf_op jit(solution)/shard_map/dot_general | solution.py:67
  432.3 11.0 %fusion.14 = f32[1536,1536]{1,0:T(8,128)} fusion(bf16[1536,1152]{1,0:T(8,128)(2,1)S(1)} %bitcast.416, bf16[3072,1152]{1,0:T(8,128)(2,1)} %get-tuple-element.29), kind=kOutput, calls=%fused_computation.37 | convolution fusion | flops 5435817984 | bytes 16515072 | tf_op jit(solution)/shard_map/dot_general | solution.py:61
  443.3 11.6 %add_convert_fusion = bf16[1536,1536]{1,0:T(8,128)(2,1)} fusion(f32[1536,1536]{1,0:T(8,128)} %fusion.14, bf16[1536,1152]{1,0:T(8,128)(2,1)S(1)} %bitcast.413, bf16[3072,1152]{1,0:T(8,128)(2,1)} %get-tuple-element.28), kind=kOutput, calls=%fused_computation.17 | convolution fusion | flops 5440536576 | bytes 21233664 | tf_op jit(solution)/shard_map/dot_general | solution.py:61
  455.4 14.6 %convolution_convert_fusion.3 = bf16[1536,1152]{1,0:T(8,128)(2,1)} fusion(bf16[3072,1536]{1,0:T(8,128)(2,1)S(1)} %bitcast.406, bf16[3072,1152]{1,0:T(8,128)(2,1)S(1)} %bitcast.422), kind=kOutput, calls=%fused_computation.22 | convolution fusion | flops 10873405440 | bytes 20054016 | tf_op jit(solution)/shard_map/dot_general | solution.py:67
  470.7 12.0 %fusion.17 = f32[1536,1536]{1,0:T(8,128)} fusion(bf16[1536,1152]{1,0:T(8,128)(2,1)} %bitcast.415, bf16[3072,1152]{1,0:T(8,128)(2,1)} %get-tuple-element.29), kind=kOutput, calls=%fused_computation.40 | convolution fusion | flops 5435817984 | bytes 16515072 | tf_op jit(solution)/shard_map/dot_general | solution.py:61
  494.6 12.3 %convert_add_fusion = f32[1536,1536]{1,0:T(8,128)S(1)} fusion(bf16[1536,1536]{1,0:T(8,128)(2,1)} %collective-permute-done.18, f32[1536,1536]{1,0:T(8,128)} %fusion.17, bf16[1536,1152]{1,0:T(8,128)(2,1)} %bitcast.412, bf16[3072,1152]{1,0:T(8,128)(2,1)} %get-tuple-element.28), kind=kOutput, calls=%fused_computation.16 | convolution fusion | flops 5442895872 | bytes 30670848 | tf_op jit(solution)/shard_map/dot_general | solution.py:61
  515.3 22.2 %reduce-scatter.12.cloned.1.call-done = bf16[1,384,1152]{2,1,0:T(8,128)(2,1)} async-done(((bf16[4,384,1152]{2,1,0:T(8,128)(2,1)}), bf16[1,384,1152]{2,1,0:T(8,128)(2,1)}) %reduce-scatter.12.cloned.1.call-update) | async-done | bytes 884752 | tf_op jit(solution)/shard_map/reduce_scatter | solution.py:184
  540.1 66.4 %reduce-scatter.10.cloned.1.call-done = bf16[1,384,1152]{2,1,0:T(8,128)(2,1)} async-done(((bf16[4,384,1152]{2,1,0:T(8,128)(2,1)}), bf16[1,384,1152]{2,1,0:T(8,128)(2,1)}) %reduce-scatter.10.cloned.1.call-update) | async-done | bytes 884752 | tf_op jit(solution)/shard_map/reduce_scatter | solution.py:184
  622.5 22.0 %collective-permute-done.20 = bf16[384,1536]{1,0:T(8,128)(2,1)S(1)} collective-permute-done((bf16[384,1536]{1,0:T(8,128)(2,1)S(1)}, bf16[384,1536]{1,0:T(8,128)(2,1)S(1)}, u32[]{:S(2)}, u32[]{:S(2)}) %collective-permute-start.20) | collective-permute-done | bytes 1179680 | tf_op jit(solution)/shard_map/ppermute | solution.py:137
  648.6 14.7 %collective-permute-start.21 = (bf16[384,1536]{1,0:T(8,128)(2,1)S(1)}, bf16[384,1536]{1,0:T(8,128)(2,1)S(1)}, u32[]{:S(2)}, u32[]{:S(2)}) collective-permute-start(bf16[384,1536]{1,0:T(8,128)(2,1)S(1)} %get-tuple-element.20), channel_id=1, source_target_pairs={{0,1},{1,0},{2,3},{3,2},{4,5},{5,4},{6,7},{7,6},{8,9},{9,8},{10,11... | collective-permute-start | bytes 3538952 | tf_op jit(solution)/shard_map/ppermute | solution.py:137
  690.9 12.0 %fusion = (f32[6,768]{1,0:T(8,128)S(1)}, f32[768,768,6]{1,0,2:T(8,128)}) fusion(f32[1,6,768,768]{2,3,1,0:T(8,128)} %copy-done, f32[6,768]{1,0:T(8,128)S(1)} %log_add_fusion, bf16[768,6,128]{0,2,1:T(8,128)(2,1)S(1)} %bitcast.387, f32[768,1024]{1,0:T(8,128)} %copy-done.10), kind=kOutput, calls=%fused_computation.3 | convolution fusion | flops 916581888 | bytes 29724672 | tf_op jit(solution)/shard_map/qkgd,skd->kgqs/dot_general | solution.py:292
  741.9 18.4 %collective-permute-start.22 = (bf16[384,1536]{1,0:T(8,128)(2,1)S(1)}, bf16[384,1536]{1,0:T(8,128)(2,1)S(1)}, u32[]{:S(2)}, u32[]{:S(2)}) collective-permute-start(bf16[384,1536]{1,0:T(8,128)(2,1)S(1)} %fusion.53), channel_id=1, source_target_pairs={{0,1},{1,0},{2,3},{3,2},{4,5},{5,4},{6,7},{7,6},{8,9},{9,8},{10,11... | collective-permute-start | bytes 3538952 | tf_op jit(solution)/shard_map/ppermute | solution.py:137
  784.6 66.6 %reduce-scatter.6.cloned.1.call-done = bf16[192,1024]{1,0:T(8,128)(2,1)} async-done(((bf16[1536,1024]{1,0:T(8,128)(2,1)}), bf16[192,1024]{1,0:T(8,128)(2,1)}) %reduce-scatter.6.cloned.1.call-update) | async-done | bytes 393232 | tf_op jit(solution)/shard_map/reduce_scatter | solution.py:194
  (397 shorter events, 301.5 us)
Async XLA Ops:
  7.2 84.4 %all-gather.9.cloned.1.call-start = ((), (), s32[]{:S(2)}) async-start(), calls=%async_computation.5 | async-start | bytes 3981312 | tf_op jit(solution)/shard_map/all_gather | solution.py:213
  10.6 133.9 %all-gather.11.cloned.1.call-start = ((), (), s32[]{:S(2)}) async-start(), calls=%async_computation.6 | async-start | bytes 2654208 | tf_op jit(solution)/shard_map/all_gather | solution.py:216
  11.3 231.4 %all-gather.15.cloned.1.call-start = ((), (), s32[]{:S(2)}) async-start(), calls=%async_computation.13 | async-start | bytes 4423680 | tf_op jit(solution)/shard_map/all_gather | solution.py:179
  39.6 245.4 %all-gather.13.cloned.1.call-start = ((), (), s32[]{:S(2)}) async-start(), calls=%async_computation.12 | async-start | bytes 4423680 | tf_op jit(solution)/shard_map/all_gather | solution.py:179
  47.7 100.7 %collective-permute-start.13 = (bf16[384,1536]{1,0:T(8,128)(2,1)}, bf16[384,1536]{1,0:T(8,128)(2,1)}, u32[]{:S(2)}, u32[]{:S(2)}) collective-permute-start(bf16[384,1536]{1,0:T(8,128)(2,1)} %bitcast.49), channel_id=1, source_target_pairs={{0,2},{1,17},{2,0},{3,19},{4,6},{5,21},{6,4},{7,23},{8,10},{9,25},... | collective-permute-start | bytes 3538952 | tf_op jit(solution)/shard_map/ppermute | solution.py:137
  69.1 286.5 %all-gather.17.cloned.1.call-start = ((), (), s32[]{:S(2)}) async-start(), calls=%async_computation.14 | async-start | bytes 4423680 | tf_op jit(solution)/shard_map/all_gather | solution.py:179
  150.4 41.7 %collective-permute-start.14 = (bf16[2,384,1536]{2,1,0:T(8,128)(2,1)S(1)}, bf16[2,384,1536]{2,1,0:T(8,128)(2,1)}, u32[]{:S(2)}, u32[]{:S(2)}) collective-permute-start(bf16[2,384,1536]{2,1,0:T(8,128)(2,1)S(1)} %pad_maximum_fusion.2), channel_id=1, source_target_pairs={{0,16},{1,3},{2,18},{3,1},{4,20},{5,7},{6,22},{7,5},{8,24},{9,11},... | collective-permute-start | bytes 7077896 | tf_op jit(solution)/shard_map/ppermute | solution.py:137
  156.8 45.6 %collective-permute-start.1 = (bf16[384,1536]{1,0:T(8,128)(2,1)S(1)}, bf16[384,1536]{1,0:T(8,128)(2,1)S(1)}, u32[]{:S(2)}, u32[]{:S(2)}) collective-permute-start(bf16[384,1536]{1,0:T(8,128)(2,1)S(1)} %get-tuple-element.25), channel_id=1, source_target_pairs={{0,2},{1,17},{2,0},{3,19},{4,6},{5,21},{6,4},{7,23},{8,10},{9,25},... | collective-permute-start | bytes 3538952 | tf_op jit(solution)/shard_map/ppermute | solution.py:137
  158.3 53.0 %collective-permute-start.15 = (bf16[384,1536]{1,0:T(8,128)(2,1)}, bf16[384,1536]{1,0:T(8,128)(2,1)S(1)}, u32[]{:S(2)}, u32[]{:S(2)}) collective-permute-start(bf16[384,1536]{1,0:T(8,128)(2,1)} %bitcast.49), channel_id=1, source_target_pairs={{0,1},{1,0},{2,3},{3,2},{4,5},{5,4},{6,7},{7,6},{8,9},{9,8},{10,11... | collective-permute-start | bytes 3538952 | tf_op jit(solution)/shard_map/ppermute | solution.py:137
  202.3 310.5 %reduce-scatter.14.cloned.1.call-start = ((), (), s32[]{:S(2)}) async-start(), calls=%async_computation.11 | async-start | bytes 4423680 | tf_op jit(solution)/shard_map/reduce_scatter | solution.py:184
  403.3 134.3 %reduce-scatter.12.cloned.1.call-start = ((), (), s32[]{:S(2)}) async-start(), calls=%async_computation.10 | async-start | bytes 4423680 | tf_op jit(solution)/shard_map/reduce_scatter | solution.py:184
  421.4 185.2 %reduce-scatter.10.cloned.1.call-start = ((), (), s32[]{:S(2)}) async-start(), calls=%async_computation.9 | async-start | bytes 4423680 | tf_op jit(solution)/shard_map/reduce_scatter | solution.py:184
  432.3 50.5 %collective-permute-start.9 = (bf16[1536,1536]{1,0:T(8,128)(2,1)}, bf16[1536,1536]{1,0:T(8,128)(2,1)}, u32[]{:S(2)}, u32[]{:S(2)}) collective-permute-start(bf16[1536,1536]{1,0:T(8,128)(2,1)} %convolution_convert_fusion), channel_id=1, source_target_pairs={{0,1},{1,0},{2,3},{3,2},{4,5},{5,4},{6,7},{7,6},{8,9},{9,8},{10,11... | collective-permute-start | bytes 14155784 | tf_op jit(solution)/shard_map/ppermute | solution.py:137
  470.0 313.0 %reduce-scatter.8.cloned.1.call-start = ((), (), s32[]{:S(2)}) async-start(), calls=%async_computation.8 | async-start | bytes 2654208 | tf_op jit(solution)/shard_map/reduce_scatter | solution.py:194
  493.2 116.0 %collective-permute-start.10 = (bf16[2,384,1536]{2,1,0:T(8,128)(2,1)}, bf16[2,384,1536]{2,1,0:T(8,128)(2,1)}, u32[]{:S(2)}, u32[]{:S(2)}) collective-permute-start(bf16[2,384,1536]{2,1,0:T(8,128)(2,1)} %bitcast.45), channel_id=1, source_target_pairs={{0,16},{1,3},{2,18},{3,1},{4,20},{5,7},{6,22},{7,5},{8,24},{9,11},... | collective-permute-start | bytes 7077896 | tf_op jit(solution)/shard_map/ppermute | solution.py:137
  508.9 105.0 %collective-permute-start.19 = (bf16[2,384,1536]{2,1,0:T(8,128)(2,1)}, bf16[2,384,1536]{2,1,0:T(8,128)(2,1)}, u32[]{:S(2)}, u32[]{:S(2)}) collective-permute-start(bf16[2,384,1536]{2,1,0:T(8,128)(2,1)} %bitcast.56), channel_id=1, source_target_pairs={{0,16},{1,3},{2,18},{3,1},{4,20},{5,7},{6,22},{7,5},{8,24},{9,11},... | collective-permute-start | bytes 7077896 | tf_op jit(solution)/shard_map/ppermute | solution.py:137
  513.8 104.4 %collective-permute-start.35 = (bf16[192,1152]{1,0:T(8,128)(2,1)S(1)}, bf16[192,1152]{1,0:T(8,128)(2,1)S(1)}, u32[]{:S(2)}, u32[]{:S(2)}) collective-permute-start(bf16[192,1152]{1,0:T(8,128)(2,1)S(1)} %dynamic-slice_bitcast_fusion), channel_id=1, source_target_pairs={{0,2},{1,3},{2,0},{3,1},{4,6},{5,7},{6,4},{7,5},{8,10},{9,11},{10,... | collective-permute-start | bytes 1327112 | tf_op jit(solution)/shard_map/ppermute | solution.py:137
  538.6 81.3 %collective-permute-start.33 = (bf16[192,1152]{1,0:T(8,128)(2,1)S(1)}, bf16[192,1152]{1,0:T(8,128)(2,1)S(1)}, u32[]{:S(2)}, u32[]{:S(2)}) collective-permute-start(bf16[192,1152]{1,0:T(8,128)(2,1)S(1)} %dynamic-slice_bitcast_fusion.1), channel_id=1, source_target_pairs={{0,2},{1,3},{2,0},{3,1},{4,6},{5,7},{6,4},{7,5},{8,10},{9,11},{10,... | collective-permute-start | bytes 1327112 | tf_op jit(solution)/shard_map/ppermute | solution.py:137
  618.4 44.9 %collective-permute-start.36 = (bf16[2,192,1152]{2,1,0:T(8,128)(2,1)S(1)}, bf16[2,192,1152]{2,1,0:T(8,128)(2,1)}, u32[]{:S(2)}, u32[]{:S(2)}) collective-permute-start(bf16[2,192,1152]{2,1,0:T(8,128)(2,1)S(1)} %pad_maximum_fusion.23), channel_id=1, source_target_pairs={{0,16},{1,17},{2,18},{3,19},{4,20},{5,21},{6,22},{7,23},{8,24},{9,... | collective-permute-start | bytes 2654216 | tf_op jit(solution)/shard_map/ppermute | solution.py:137
  620.1 44.6 %collective-permute-start.34 = (bf16[2,192,1152]{2,1,0:T(8,128)(2,1)S(1)}, bf16[2,192,1152]{2,1,0:T(8,128)(2,1)}, u32[]{:S(2)}, u32[]{:S(2)}) collective-permute-start(bf16[2,192,1152]{2,1,0:T(8,128)(2,1)S(1)} %pad_maximum_fusion.22), channel_id=1, source_target_pairs={{0,16},{1,17},{2,18},{3,19},{4,20},{5,21},{6,22},{7,23},{8,24},{9,... | collective-permute-start | bytes 2654216 | tf_op jit(solution)/shard_map/ppermute | solution.py:137
  620.9 58.0 %collective-permute-start.32 = (bf16[2,192,1152]{2,1,0:T(8,128)(2,1)S(1)}, bf16[2,192,1152]{2,1,0:T(8,128)(2,1)S(1)}, u32[]{:S(2)}, u32[]{:S(2)}) collective-permute-start(bf16[2,192,1152]{2,1,0:T(8,128)(2,1)S(1)} %pad_maximum_fusion.21), channel_id=1, source_target_pairs={{0,16},{1,17},{2,18},{3,19},{4,20},{5,21},{6,22},{7,23},{8,24},{9,... | collective-permute-start | bytes 2654216 | tf_op jit(solution)/shard_map/ppermute | solution.py:137
  663.2 102.0 %collective-permute-start.12 = (bf16[384,1536]{1,0:T(8,128)(2,1)}, bf16[384,1536]{1,0:T(8,128)(2,1)}, u32[]{:S(2)}, u32[]{:S(2)}) collective-permute-start(bf16[384,1536]{1,0:T(8,128)(2,1)} %get-tuple-element.37), channel_id=1, source_target_pairs={{0,1},{1,0},{2,3},{3,2},{4,5},{5,4},{6,7},{7,6},{8,9},{9,8},{10,11... | collective-permute-start | bytes 3538952 | tf_op jit(solution)/shard_map/ppermute | solution.py:137
  686.4 164.7 %reduce-scatter.6.cloned.1.call-start = ((), (), s32[]{:S(2)}) async-start(), calls=%async_computation.7 | async-start | bytes 3538944 | tf_op jit(solution)/shard_map/reduce_scatter | solution.py:194
  783.0 71.1 %collective-permute-start.30 = (bf16[192,768]{1,0:T(8,128)(2,1)}, bf16[192,768]{1,0:T(8,128)(2,1)S(1)}, u32[]{:S(2)}, u32[]{:S(2)}) collective-permute-start(bf16[192,768]{1,0:T(8,128)(2,1)} %reduce-scatter.8.cloned.1.call-done), channel_id=1, source_target_pairs={{0,16},{1,17},{2,18},{3,19},{4,20},{5,21},{6,22},{7,23},{8,24},{9,... | collective-permute-start | bytes 884744 | tf_op jit(solution)/shard_map/ppermute | solution.py:137
  (97 other events, 1130.5 us)
Sparse Core Ops, SparseCore 0:
  10.7 80.7 all-gather.8
  93.7 50.6 all-gather.10
  146.0 68.4 all-gather.14
  216.5 68.5 all-gather.12
  287.0 68.5 all-gather.16
  403.4 65.0 reduce-scatter.13
  470.8 66.6 reduce-scatter.11
  539.8 66.6 reduce-scatter.9
  686.5 87.1 reduce-scatter.7
  777.1 73.9 reduce-scatter.5

commit v2 on v1

--- a/solution.py
+++ b/solution.py
@@ -87,7 +87,11 @@
             for t in range(2)
         ]
 
-    return {
+    shifts = {
+        step: table(lambda g, d, t: (g, (d + 2 * step) % dp_count, t))
+        for step in range(1, dp_count // 2)
+    }
+    return shifts | {
         "x": table(lambda g, d, t: (g, d ^ 1, t)),
         "y": table(lambda g, d, t: (g ^ 1, d, t)),
         "t": table(lambda g, d, t: (g, d, t ^ 1)),
@@ -119,6 +123,7 @@
     line = dp_count // 2
     dp_index = lax.axis_index("dp")
     x_index = dp_index % 2
+    z_index = dp_index // 2
     y_index = lax.axis_index("group")
     core = lax.axis_index("tensor")
     table = routes(dp_count)
@@ -170,20 +175,66 @@
         came = send(total[1].astype(bf16), "first")
         return total[0] + came.astype(f32)
 
-    def ffn_gather(weight):
+    def after(value, *others):
+        return lax.optimization_barrier((value, *others))[0]
+
+    def ffn_parts(weight):
         padded = jnp.pad(weight, ((0, 0), (0, 4 * quarter - ffn_cols)))
-        parts = padded.reshape(rows, 4, quarter).transpose(1, 0, 2)
-        mine = pick(parts, x_index * 2 + y_index)
-        came = send(pick(parts, (1 - x_index) * 2 + y_index), "x")
-        pair = jnp.stack(in_order(x_index, mine, came))
+        return padded.reshape(rows, 4, quarter).transpose(1, 0, 2)
+
+    def ffn_pair(parts):
+        mine = jnp.concatenate([pick(p, x_index * 2 + y_index) for p in parts], axis=1)
+        other = jnp.concatenate([pick(p, (1 - x_index) * 2 + y_index) for p in parts], axis=1)
+        return jnp.stack(in_order(x_index, mine, send(other, "x")))
+
+    def ffn_gather(pair):
         full = lax.all_gather(pair, "dp", axis=0, axis_index_groups=line_groups)
-        return full.reshape(d_model, quarter)
+        return full.reshape(d_model, pair.shape[-1])
+
+    def put(whole, piece, index):
+        return lax.dynamic_update_slice(whole, piece.reshape((1,) + piece.shape), index)
+
+    part_rows = rows // 2
+
+    def attn_line(weight):
+        mine = lax.dynamic_slice_in_dim(weight, y_index * part_rows, part_rows, 0)
+        whole = jnp.zeros((line,) + mine.shape, bf16)
+        came = [mine] + [send(mine, step) for step in range(1, line)]
+        for step, piece in enumerate(came):
+            whole = put(whole, piece, ((z_index - step) % line, 0, 0))
+        return whole
+
+    def attn_square(blocks):
+        cols = blocks.shape[-1]
+        whole = jnp.zeros((line, 2, 2, part_rows, cols), bf16)
+        cut = line // 2
+        low, high = blocks[:cut], blocks[cut:]
+        low_near = send(low, "x")
+        high_near = send(high, "y")
+        low_far = send(jnp.stack([low, low_near]), "y")
+        high_far = send(jnp.stack([high, high_near]), "x")
+
+        def place(whole, piece, z, x, y):
+            return lax.dynamic_update_slice(whole, piece[:, None, None], (z, x, y, 0, 0))
+
+        x, y = x_index, y_index
+        whole = place(whole, low, 0, x, y)
+        whole = place(whole, low_near, 0, 1 - x, y)
+        whole = place(whole, low_far[0], 0, x, 1 - y)
+        whole = place(whole, low_far[1], 0, 1 - x, 1 - y)
+        whole = place(whole, high, cut, x, y)
+        whole = place(whole, high_near, cut, x, 1 - y)
+        whole = place(whole, high_far[0], cut, 1 - x, y)
+        whole = place(whole, high_far[1], cut, 1 - x, 1 - y)
+        return whole.reshape(d_model, cols)
 
     def ffn_scatter(grad):
         parts = grad.astype(bf16).reshape(line, 2 * rows, quarter)
-        summed = lax.psum_scatter(
+        return lax.psum_scatter(
             parts, "dp", scatter_dimension=0, axis_index_groups=line_groups
         ).reshape(2, rows, quarter)
+
+    def ffn_swap(summed):
         came = send(pick(summed, 1 - x_index), "x")
         pair = jnp.stack(in_order(x_index, pick(summed, x_index), came))
         low, high = in_order(y_index, pair, send(pair, "y"))
@@ -191,10 +242,25 @@
         return whole[:, :ffn_cols].astype(f32)
 
     def attn_scatter(grad):
-        summed = lax.psum_scatter(
-            grad.astype(bf16), "dp", scatter_dimension=0, tiled=True
-        )
-        return summed.astype(f32) + send(summed, "y").astype(f32)
+        cols = grad.shape[-1]
+        cut = line // 2
+        view = grad.astype(bf16).reshape(line, 2, 2, part_rows, cols)
+
+        def take(value, axis, index):
+            return lax.dynamic_index_in_dim(value, index, axis, keepdims=False)
+
+        low, high = view[:cut], view[cut:]
+        low = take(low, 1, x_index).astype(f32) + send(take(low, 1, 1 - x_index), "x").astype(f32)
+        high = take(high, 2, y_index).astype(f32) + send(take(high, 2, 1 - y_index), "y").astype(f32)
+        low, high = low.astype(bf16), high.astype(bf16)
+        low = take(low, 1, y_index).astype(f32) + send(take(low, 1, 1 - y_index), "y").astype(f32)
+        high = take(high, 1, x_index).astype(f32) + send(take(high, 1, 1 - x_index), "x").astype(f32)
+        blocks = jnp.concatenate([low, high]).astype(bf16)
+        total = pick(blocks, z_index).astype(f32)
+        for step in range(1, line):
+            total = total + send(pick(blocks, (z_index + step) % line), step).astype(f32)
+        mine = total.astype(bf16)
+        return jnp.concatenate(in_order(y_index, mine, send(mine, "y"))).astype(f32)
 
     stream = inputs.astype(f32)
     segment, position = layout(lengths[0])
@@ -210,15 +276,18 @@
     query_cols = head_count * HD
     key_cols = kv_count * HD
     qkv_cols = query_cols + 2 * key_cols
-    qkv_full = lax.all_gather(
-        jnp.concatenate([w_query, w_key, w_value, gains], axis=1), "dp", axis=0, tiled=True
-    )
-    out_full = lax.all_gather(w_out, "dp", axis=0, tiled=True)
-    gate_full = ffn_gather(w_gate)
-    up_full = ffn_gather(w_up)
-    down_full = ffn_gather(w_down)
+    gate_up_pair = ffn_pair([ffn_parts(w_gate), ffn_parts(w_up)])
+    qkv_line = attn_line(jnp.concatenate([w_query, w_key, w_value, gains], axis=1))
+    out_line = attn_line(after(w_out, qkv_line))
+    qkv_full = attn_square(after(qkv_line, gate_up_pair))
+    out_full = attn_square(after(out_line, qkv_full))
+    down_pair = ffn_pair([ffn_parts(after(w_down, qkv_full))])
+    gate_up_full = ffn_gather(gate_up_pair)
+    down_full = ffn_gather(after(down_pair, gate_up_pair))
+    gate_full = gate_up_full[:, :quarter]
+    up_full = gate_up_full[:, quarter:]
     cot_half = my_half(cotangent)
-    cot_all = square_gather(cot_half)
+    cot_all = square_gather(after(cot_half, out_full))
 
     gain_one = qkv_full[:, qkv_cols].astype(f32)
     gain_two = qkv_full[:, qkv_cols + 1].astype(f32)
@@ -258,7 +327,7 @@
     sigmoid_gate = jax.nn.sigmoid(gate_pre)
     swish_gate = gate_pre * sigmoid_gate
     hidden = (swish_gate * up_pre).astype(bf16)
-    down_grad = ffn_scatter(outer_dot(cot_all, hidden))
+    down_sum = ffn_scatter(outer_dot(cot_all, hidden))
     d_hidden = plain_dot(cot_all, down_full)
     d_gate = (d_hidden * up_pre * sigmoid_gate * (1.0 + gate_pre * (1.0 - sigmoid_gate))).astype(
         bf16
@@ -270,8 +339,8 @@
         return trans_dot(d_gate[part], gate_full) + trans_dot(d_up[part], up_full)
 
     d_h_two = square_scatter(entry(slice(0, mid)), entry(slice(mid, None)))
-    gate_grad = ffn_scatter(outer_dot(h_two, d_gate))
-    up_grad = ffn_scatter(outer_dot(h_two, d_up))
+    gate_sum = ffn_scatter(outer_dot(h_two, d_gate))
+    up_sum = ffn_scatter(outer_dot(h_two, d_up))
     ffn_total = square_scatter(
         trans_dot(hidden[:mid], down_full), trans_dot(hidden[mid:], down_full)
     )
@@ -311,6 +380,9 @@
     d_qkv = jnp.concatenate([d_query, d_key, d_value], axis=1)
     qkv_grad = attn_scatter(outer_dot(h_one, d_qkv))
     entry_one = trans_dot(d_qkv, qkv_full)
+    down_grad = ffn_swap(after(down_sum, d_out_low))
+    gate_grad = ffn_swap(after(gate_sum, entry_one))
+    up_grad = ffn_swap(after(up_sum, qkv_grad))
     d_h_one = my_half(entry_one) + send(other_half(entry_one).astype(bf16), "t").astype(f32)
     half_inv = my_half(inv_one)
     norm_one = my_half(stream) * half_inv

time: 877 us -> 741 us (0.84)
  waiting for transfers between devices: 384 us -> 199 us
  local copies, waits for them, and re-layouts: 87.7 us -> 120 us
  other arithmetic: 66.3 us -> 81.8 us
  matrix products: 240 us -> 225 us
  starting transfers between devices: 76.5 us -> 90.3 us
    reduce_scatter x3, waiting for transfers between devices: 88.7 us -> 0.04 us  [ffn_scatter(): lax.psum_scatter(parts, 'dp', scatter_dimension=0, axis_index_groups=line...]
    ppermute x34 -> x61, waiting for transfers between devices: 114 us -> 191 us  [send(): return lax.ppermute(value, AXES, table[route])]
    all_gather x3 -> x2, waiting for transfers between devices: 77.1 us -> 0.01 us  [ffn_gather(): full = lax.all_gather(pair, 'dp', axis=0, axis_index_groups=line_groups)]
    reduce_scatter x2 -> x0, waiting for transfers between devices: 66.6 us -> none  [attn_scatter(): lax.psum_scatter(grad.astype(bf16), 'dp', scatter_dimension=0, tiled=True)]
    all_gather x2 -> x0, waiting for transfers between devices: 33.1 us -> none  [the longest x1 22.2 us: local(): lax.all_gather(jnp.concatenate([w_query, w_key, w_value, gains], axis=1),...]
    dynamic_update_slice x0 -> x23, local copies, waits for them, and re-layouts: none -> 12.9 us  [the longest x7 7.41 us: put(): lax.dynamic_update_slice(whole, piece.reshape((1,) + piece.shape), index)]
    ppermute x34 -> x61, starting transfers between devices: 70.9 us -> 81.4 us  [send(): return lax.ppermute(value, AXES, table[route])]
    unnamed x164 -> x184, local copies, waits for them, and re-layouts: 37.1 us -> 43.3 us
  transfers between devices with their start and end apart: 47 -> 69, of which waited for: 21 -> 28; matrix products, arithmetic and copies ran while one was open for 38% -> 47% of each run, Pallas kernels for 0% -> 0%
where the time goes in v2:
time: 741 us; the launch traced here: 731 us
  matrix products  225 us (30%)
  waiting for transfers between devices  199 us (27%)
  local copies, waits for them, and re-layouts  120 us (16%)
  starting transfers between devices  90.3 us (12%)
  other arithmetic  81.8 us (11%)
  between operations  15.9 us (2%)
    ppermute x61, waiting for transfers between devices, send(): return lax.ppermute(value, AXES, table[route])  191 us
    ppermute x61, starting transfers between devices, send(): return lax.ppermute(value, AXES, table[route])  81.4 us
    dot_general x8, matrix products, trans_dot(): lax.dot_general(left_side, right_side, (((1,), (1,)), ((), ())), preferre...  70 us
    dot_general x5, matrix products, plain_dot(): return jnp.dot(left_side, right_side, preferred_element_type=jnp.float32)  69.1 us
    dot_general x5, matrix products, outer_dot(): lax.dot_general(left_side, right_side, (((0,), (0,)), ((), ())), preferre...  60.8 us
    unnamed x184, local copies, waits for them, and re-layouts  43.3 us
  transfers between devices with their start and end apart: 69, of which 28 were waited for; matrix products, arithmetic and copies ran while one was open for 47% of the time, Pallas kernels for 0%

profile of v2, /device:TPU:0, one launch (start us, length us, event | category | flops | bytes accessed | tf_op | source)
XLA Modules:
  0.0 731.2 jit_solution(11844036942741049264)
XLA Ops:
  23.9 7.5 %constant_dynamic-slice_fusion.15 = (bf16[192,1,1152]{2,1,0:T(2,128)(2,1)}, bf16[192,1,1152]{2,1,0:T(2,128)(2,1)S(1)}, bf16[192,1,1152]{2,1,0:T(2,128)(2,1)S(1)}, bf16[192,1,1152]{2,1,0:T(2,128)(2,1)}) fusion(bf16[192,4,1152]{2,1,0:T(4,128)(2,1)} %reshape.519, s32[]{:T(128)S(6)} %select_n.341, s32[]{:T(128)S(6)} %select_n.342, ...), kind=kLoop, calls=%fused_computation.368 | loop fusion | bytes 3538952 | tf_op jit(solution)/shard_map/dynamic-slice.1
  77.0 14.6 %collective-permute-done.5 = bf16[2,2,96,1152]{3,2,1,0:T(8,128)(2,1)S(1)} collective-permute-done((bf16[2,2,96,1152]{3,2,1,0:T(8,128)(2,1)S(1)}, bf16[2,2,96,1152]{3,2,1,0:T(8,128)(2,1)S(1)}, u32[]{:S(2)}, u32[]{:S(2)}) %collective-permute-start.5) | collective-permute-done | bytes 884768 | tf_op jit(solution)/shard_map/ppermute | solution.py:142
  181.3 24.0 %collective-permute-done.16 = bf16[384,1536]{1,0:T(8,128)(2,1)S(1)} collective-permute-done((bf16[384,1536]{1,0:T(8,128)(2,1)}, bf16[384,1536]{1,0:T(8,128)(2,1)S(1)}, u32[]{:S(2)}, u32[]{:S(2)}) %collective-permute-start.16) | collective-permute-done | bytes 1179680 | tf_op jit(solution)/shard_map/ppermute | solution.py:142
  218.4 19.4 %collective-permute-done.17 = bf16[2,384,1536]{2,1,0:T(8,128)(2,1)S(1)} collective-permute-done((bf16[2,384,1536]{2,1,0:T(8,128)(2,1)S(1)}, bf16[2,384,1536]{2,1,0:T(8,128)(2,1)S(1)}, u32[]{:S(2)}, u32[]{:S(2)}) %collective-permute-start.17) | collective-permute-done | bytes 2359328 | tf_op jit(solution)/shard_map/ppermute | solution.py:142
  251.2 18.1 %fusion.30 = f32[3072,1152]{1,0:T(8,128)} fusion(bf16[3072,1536]{1,0:T(8,128)(2,1)} %fusion.68, bf16[1536,2304]{1,0:T(8,128)(2,1)} %bitcast.586), kind=kOutput, calls=%fused_computation.53 | convolution fusion | flops 10871635968 | bytes 27131904 | tf_op jit(solution)/shard_map/dot_general | solution.py:57
  269.2 16.8 %fusion.34 = f32[3072,1152]{1,0:T(8,128)} fusion(bf16[3072,1536]{1,0:T(8,128)(2,1)} %fusion.68, bf16[1536,2304]{1,0:T(8,128)(2,1)S(1)} %bitcast.590), kind=kOutput, calls=%fused_computation.57 | convolution fusion | flops 10871635968 | bytes 27131904 | tf_op jit(solution)/shard_map/dot_general | solution.py:57
  286.0 29.6 %multiply_convert_fusion = (bf16[3072,1152]{1,0:T(8,128)(2,1)}, bf16[3072,1152]{1,0:T(8,128)(2,1)}, bf16[3072,1152]{1,0:T(8,128)(2,1)}) fusion(f32[3072,1152]{1,0:T(8,128)} %fusion.34, f32[3072,1152]{1,0:T(8,128)} %fusion.30, bf16[3072,1536]{1,0:T(8,128)(2,1)} %copy-done.48, bf16[1536,1152]{1,0:T(8,128)(2,1)} %bitcast.594), kind=kOutput, calls=%fused_computation.7 | convolution fusion | flops 10924720128 | bytes 62521344 | tf_op jit(solution)/shard_map/dot_general | solution.py:57
  315.6 18.3 %convolution_convert_fusion.1 = bf16[1536,1152]{1,0:T(8,128)(2,1)} fusion(bf16[3072,1536]{1,0:T(8,128)(2,1)} %copy-done.48, bf16[3072,1152]{1,0:T(8,128)(2,1)} %get-tuple-element.50), kind=kOutput, calls=%fused_computation.20 | convolution fusion | flops 10873405440 | bytes 20054016 | tf_op jit(solution)/shard_map/dot_general | solution.py:67
  335.9 10.2 %convolution_convert_fusion = bf16[1536,1536]{1,0:T(8,128)(2,1)} fusion(bf16[1536,1152]{1,0:T(8,128)(2,1)S(1)} %bitcast.595, bf16[3072,1152]{1,0:T(8,128)(2,1)} %get-tuple-element.50), kind=kOutput, calls=%fused_computation.19 | convolution fusion | flops 5438177280 | bytes 11796480 | tf_op jit(solution)/shard_map/dot_general | solution.py:61
  346.1 9.7 %fusion.14 = f32[1536,1536]{1,0:T(8,128)S(1)} fusion(bf16[3072,1152]{1,0:T(8,128)(2,1)} %get-tuple-element.49, bf16[1536,2304]{1,0:T(8,128)(2,1)} %bitcast.587), kind=kOutput, calls=%fused_computation.37 | convolution fusion | flops 5435817984 | bytes 16515072 | tf_op jit(solution)/shard_map/dot_general | solution.py:61
  355.8 10.4 %add_convert_fusion = bf16[1536,1536]{1,0:T(8,128)(2,1)} fusion(f32[1536,1536]{1,0:T(8,128)S(1)} %fusion.14, bf16[3072,1152]{1,0:T(8,128)(2,1)} %get-tuple-element.48, bf16[1536,2304]{1,0:T(8,128)(2,1)S(1)} %bitcast.593), kind=kOutput, calls=%fused_computation.17 | convolution fusion | flops 5440536576 | bytes 21233664 | tf_op jit(solution)/shard_map/dot_general | solution.py:61
  366.6 16.3 %convolution_convert_fusion.3 = bf16[1536,1152]{1,0:T(8,128)(2,1)} fusion(bf16[3072,1536]{1,0:T(8,128)(2,1)} %fusion.68, bf16[3072,1152]{1,0:T(8,128)(2,1)S(1)} %bitcast.599), kind=kOutput, calls=%fused_computation.22 | convolution fusion | flops 10873405440 | bytes 20054016 | tf_op jit(solution)/shard_map/dot_general | solution.py:67
  384.3 11.4 %fusion.17 = f32[1536,1536]{1,0:T(8,128)} fusion(bf16[3072,1152]{1,0:T(8,128)(2,1)} %get-tuple-element.49, bf16[1536,2304]{1,0:T(8,128)(2,1)} %bitcast.588), kind=kOutput, calls=%fused_computation.40 | convolution fusion | flops 5435817984 | bytes 16515072 | tf_op jit(solution)/shard_map/dot_general | solution.py:61
  395.8 8.4 %convert_add_fusion.1 = f32[1536,1536]{1,0:T(8,128)S(1)} fusion(bf16[1536,1536]{1,0:T(8,128)(2,1)} %collective-permute-done.22, bf16[1536,1152]{1,0:T(8,128)(2,1)S(1)} %bitcast.596, bf16[3072,1152]{1,0:T(8,128)(2,1)S(1)} %bitcast.601), kind=kOutput, calls=%fused_computation.18 | convolution fusion | flops 5440536576 | bytes 21233664 | tf_op jit(solution)/shard_map/dot_general | solution.py:61
  409.6 13.3 %convert_add_fusion = f32[1536,1536]{1,0:T(8,128)S(1)} fusion(bf16[1536,1536]{1,0:T(8,128)(2,1)} %collective-permute-done.31, f32[1536,1536]{1,0:T(8,128)} %fusion.17, bf16[3072,1152]{1,0:T(8,128)(2,1)} %get-tuple-element.48, bf16[1536,2304]{1,0:T(8,128)(2,1)} %bitcast.589), kind=kOutput, calls=%fused_computation.16 | convolution fusion | flops 5442895872 | bytes 30670848 | tf_op jit(solution)/shard_map/dot_general | solution.py:61
  425.5 19.9 %convolution_convert_fusion.2 = bf16[1536,1152]{1,0:T(8,128)(2,1)} fusion(bf16[3072,1536]{1,0:T(8,128)(2,1)} %fusion.68, bf16[3072,1152]{1,0:T(8,128)(2,1)} %get-tuple-element.48), kind=kOutput, calls=%fused_computation.21 | convolution fusion | flops 10873405440 | bytes 20054016 | tf_op jit(solution)/shard_map/dot_general | solution.py:67
  453.4 9.0 %collective-permute-done.32 = bf16[2,384,1536]{2,1,0:T(8,128)(2,1)} collective-permute-done((bf16[2,384,1536]{2,1,0:T(8,128)(2,1)}, bf16[2,384,1536]{2,1,0:T(8,128)(2,1)}, u32[]{:S(2)}, u32[]{:S(2)}) %collective-permute-start.32) | collective-permute-done | bytes 2359328 | tf_op jit(solution)/shard_map/ppermute | solution.py:142
  473.2 10.4 %collective-permute-done.33 = bf16[384,1536]{1,0:T(8,128)(2,1)S(1)} collective-permute-done((bf16[384,1536]{1,0:T(8,128)(2,1)S(1)}, bf16[384,1536]{1,0:T(8,128)(2,1)S(1)}, u32[]{:S(2)}, u32[]{:S(2)}) %collective-permute-start.33) | collective-permute-done | bytes 1179680 | tf_op jit(solution)/shard_map/ppermute | solution.py:142
  484.3 11.8 %collective-permute-done.24 = bf16[384,1536]{1,0:T(8,128)(2,1)S(1)} collective-permute-done((bf16[384,1536]{1,0:T(8,128)(2,1)S(1)}, bf16[384,1536]{1,0:T(8,128)(2,1)S(1)}, u32[]{:S(2)}, u32[]{:S(2)}) %collective-permute-start.24) | collective-permute-done | bytes 1179680 | tf_op jit(solution)/shard_map/ppermute | solution.py:142
  498.6 12.1 %collective-permute-start.34 = (bf16[384,1536]{1,0:T(8,128)(2,1)S(1)}, bf16[384,1536]{1,0:T(8,128)(2,1)S(1)}, u32[]{:S(2)}, u32[]{:S(2)}) collective-permute-start(bf16[384,1536]{1,0:T(8,128)(2,1)S(1)} %get-tuple-element.38), channel_id=1, source_target_pairs={{0,1},{1,0},{2,3},{3,2},{4,5},{5,4},{6,7},{7,6},{8,9},{9,8},{10,11... | collective-permute-start | bytes 3538952 | tf_op jit(solution)/shard_map/ppermute | solution.py:142
  520.8 7.7 %fusion = (f32[6,768]{1,0:T(8,128)S(1)}, f32[768,768,6]{1,0,2:T(8,128)}) fusion(f32[1,6,768,768]{2,3,1,0:T(8,128)S(1)} %bitcast.529, f32[6,768]{1,0:T(8,128)S(1)} %log_add_fusion, bf16[768,6,128]{0,2,1:T(8,128)(2,1)S(1)} %bitcast.554, f32[768,1024]{1,0:T(8,128)} %copy-done.8), kind=kOutput, calls=%fused_computation.3 | convolution fusion | flops 916581888 | bytes 29724672 | tf_op jit(solution)/shard_map/qkgd,skd->kgqs/dot_general | solution.py:361
  589.8 9.8 %collective-permute-done.42 = bf16[2,2,96,1024]{3,2,0,1:T(8,128)(2,1)S(1)} collective-permute-done((bf16[2,2,96,1024]{3,2,0,1:T(8,128)(2,1)S(1)}, bf16[2,2,96,1024]{3,2,0,1:T(8,128)(2,1)S(1)}, u32[]{:S(2)}, u32[]{:S(2)}) %collective-permute-start.42) | collective-permute-done | bytes 786464 | tf_op jit(solution)/shard_map/ppermute | solution.py:142
  603.7 24.0 %collective-permute-done.51 = bf16[2,96,768]{2,1,0:T(8,128)(2,1)S(1)} collective-permute-done((bf16[2,96,768]{2,1,0:T(8,128)(2,1)S(1)}, bf16[2,96,768]{2,1,0:T(8,128)(2,1)S(1)}, u32[]{:S(2)}, u32[]{:S(2)}) %collective-permute-start.51) | collective-permute-done | bytes 294944 | tf_op jit(solution)/shard_map/ppermute | solution.py:142
  706.5 15.6 %collective-permute-done.61 = bf16[2,192,1152]{2,1,0:T(8,128)(2,1)S(1)} collective-permute-done((bf16[2,192,1152]{2,1,0:T(8,128)(2,1)S(1)}, bf16[2,192,1152]{2,1,0:T(8,128)(2,1)S(1)}, u32[]{:S(2)}, u32[]{:S(2)}) %collective-permute-start.61) | collective-permute-done | bytes 884768 | tf_op jit(solution)/shard_map/ppermute | solution.py:142
  (519 shorter events, 366.9 us)
Async XLA Ops:
  7.2 244.0 %all-gather.5.cloned.1.call-start = ((), (), s32[]{:S(2)}) async-start(), calls=%async_computation.6 | async-start | bytes 8847360 | tf_op jit(solution)/shard_map/all_gather | solution.py:191
  62.4 223.7 %all-gather.7.cloned.1.call-start = ((), (), s32[]{:S(2)}) async-start(), calls=%async_computation.7 | async-start | bytes 4423680 | tf_op jit(solution)/shard_map/all_gather | solution.py:191
  99.2 38.7 %collective-permute-start.13 = (bf16[2,96,768]{2,1,0:T(8,128)(2,1)}, bf16[2,96,768]{2,1,0:T(8,128)(2,1)}, u32[]{:S(2)}, u32[]{:S(2)}) collective-permute-start(bf16[2,96,768]{2,1,0:T(8,128)(2,1)} %get-tuple-element.122), channel_id=1, source_target_pairs={{0,16},{1,17},{2,18},{3,19},{4,20},{5,21},{6,22},{7,23},{8,24},{9,... | collective-permute-start | bytes 884744 | tf_op jit(solution)/shard_map/ppermute | solution.py:142
  100.7 34.3 %collective-permute-start.11 = (bf16[2,96,768]{2,1,0:T(8,128)(2,1)}, bf16[2,96,768]{2,1,0:T(8,128)(2,1)}, u32[]{:S(2)}, u32[]{:S(2)}) collective-permute-start(bf16[2,96,768]{2,1,0:T(8,128)(2,1)} %get-tuple-element.123), channel_id=1, source_target_pairs={{0,2},{1,3},{2,0},{3,1},{4,6},{5,7},{6,4},{7,5},{8,10},{9,11},{10,... | collective-permute-start | bytes 884744 | tf_op jit(solution)/shard_map/ppermute | solution.py:142
  170.8 41.8 %collective-permute-start.27 = (bf16[2,384,1536]{2,1,0:T(8,128)(2,1)}, bf16[2,384,1536]{2,1,0:T(8,128)(2,1)}, u32[]{:S(2)}, u32[]{:S(2)}) collective-permute-start(bf16[2,384,1536]{2,1,0:T(8,128)(2,1)} %pad_maximum_fusion.2), channel_id=1, source_target_pairs={{0,16},{1,3},{2,18},{3,1},{4,20},{5,7},{6,22},{7,5},{8,24},{9,11},... | collective-permute-start | bytes 7077896 | tf_op jit(solution)/shard_map/ppermute | solution.py:142
  181.2 270.6 %reduce-scatter.8.cloned.1.call-start = ((), (), s32[]{:S(2)}) async-start(), calls=%async_computation.5 | async-start | bytes 4423680 | tf_op jit(solution)/shard_map/reduce_scatter | solution.py:233
  181.2 36.9 %collective-permute-start.28 = (bf16[384,1536]{1,0:T(8,128)(2,1)S(1)}, bf16[384,1536]{1,0:T(8,128)(2,1)S(1)}, u32[]{:S(2)}, u32[]{:S(2)}) collective-permute-start(bf16[384,1536]{1,0:T(8,128)(2,1)S(1)} %copy-done.9), channel_id=1, source_target_pairs={{0,1},{1,0},{2,3},{3,2},{4,5},{5,4},{6,7},{7,6},{8,9},{9,8},{10,11... | collective-permute-start | bytes 3538952 | tf_op jit(solution)/shard_map/ppermute | solution.py:142
  206.9 31.0 %collective-permute-start.17 = (bf16[2,384,1536]{2,1,0:T(8,128)(2,1)S(1)}, bf16[2,384,1536]{2,1,0:T(8,128)(2,1)S(1)}, u32[]{:S(2)}, u32[]{:S(2)}) collective-permute-start(bf16[2,384,1536]{2,1,0:T(8,128)(2,1)S(1)} %pad_maximum_fusion), channel_id=1, source_target_pairs={{0,16},{1,3},{2,18},{3,1},{4,20},{5,7},{6,22},{7,5},{8,24},{9,11},... | collective-permute-start | bytes 7077896 | tf_op jit(solution)/shard_map/ppermute | solution.py:142
  208.4 34.5 %collective-permute-start.18 = (bf16[384,1536]{1,0:T(8,128)(2,1)}, bf16[384,1536]{1,0:T(8,128)(2,1)S(1)}, u32[]{:S(2)}, u32[]{:S(2)}) collective-permute-start(bf16[384,1536]{1,0:T(8,128)(2,1)} %get-tuple-element.41), channel_id=1, source_target_pairs={{0,1},{1,0},{2,3},{3,2},{4,5},{5,4},{6,7},{7,6},{8,9},{9,8},{10,11... | collective-permute-start | bytes 3538952 | tf_op jit(solution)/shard_map/ppermute | solution.py:142
  212.6 32.5 %collective-permute-start.30 = (bf16[2,384,1536]{2,1,0:T(8,128)(2,1)}, bf16[2,384,1536]{2,1,0:T(8,128)(2,1)S(1)}, u32[]{:S(2)}, u32[]{:S(2)}) collective-permute-start(bf16[2,384,1536]{2,1,0:T(8,128)(2,1)} %collective-permute-done.27), channel_id=1, source_target_pairs={{0,1},{1,0},{2,3},{3,2},{4,5},{5,4},{6,7},{7,6},{8,9},{9,8},{10,11... | collective-permute-start | bytes 7077896 | tf_op jit(solution)/shard_map/ppermute | solution.py:142
  333.9 228.9 %reduce-scatter.4.cloned.1.call-start = ((), (), s32[]{:S(2)}) async-start(), calls=%async_computation.3 | async-start | bytes 4423680 | tf_op jit(solution)/shard_map/reduce_scatter | solution.py:233
  346.1 49.7 %collective-permute-start.22 = (bf16[1536,1536]{1,0:T(8,128)(2,1)}, bf16[1536,1536]{1,0:T(8,128)(2,1)}, u32[]{:S(2)}, u32[]{:S(2)}) collective-permute-start(bf16[1536,1536]{1,0:T(8,128)(2,1)} %convolution_convert_fusion), channel_id=1, source_target_pairs={{0,1},{1,0},{2,3},{3,2},{4,5},{5,4},{6,7},{7,6},{8,9},{9,8},{10,11... | collective-permute-start | bytes 14155784 | tf_op jit(solution)/shard_map/ppermute | solution.py:142
  366.2 43.4 %collective-permute-start.31 = (bf16[1536,1536]{1,0:T(8,128)(2,1)}, bf16[1536,1536]{1,0:T(8,128)(2,1)}, u32[]{:S(2)}, u32[]{:S(2)}) collective-permute-start(bf16[1536,1536]{1,0:T(8,128)(2,1)} %add_convert_fusion), channel_id=1, source_target_pairs={{0,1},{1,0},{2,3},{3,2},{4,5},{5,4},{6,7},{7,6},{8,9},{9,8},{10,11... | collective-permute-start | bytes 14155784 | tf_op jit(solution)/shard_map/ppermute | solution.py:142
  383.0 307.4 %reduce-scatter.6.cloned.1.call-start = ((), (), s32[]{:S(2)}) async-start(), calls=%async_computation.4 | async-start | bytes 4423680 | tf_op jit(solution)/shard_map/reduce_scatter | solution.py:233
  408.1 59.3 %collective-permute-start.23 = (bf16[2,384,1536]{2,1,0:T(8,128)(2,1)S(1)}, bf16[2,384,1536]{2,1,0:T(8,128)(2,1)}, u32[]{:S(2)}, u32[]{:S(2)}) collective-permute-start(bf16[2,384,1536]{2,1,0:T(8,128)(2,1)S(1)} %bitcast.565), channel_id=1, source_target_pairs={{0,16},{1,3},{2,18},{3,1},{4,20},{5,7},{6,22},{7,5},{8,24},{9,11},... | collective-permute-start | bytes 7077896 | tf_op jit(solution)/shard_map/ppermute | solution.py:142
  424.9 37.5 %collective-permute-start.32 = (bf16[2,384,1536]{2,1,0:T(8,128)(2,1)}, bf16[2,384,1536]{2,1,0:T(8,128)(2,1)}, u32[]{:S(2)}, u32[]{:S(2)}) collective-permute-start(bf16[2,384,1536]{2,1,0:T(8,128)(2,1)} %bitcast.93), channel_id=1, source_target_pairs={{0,16},{1,3},{2,18},{3,1},{4,20},{5,7},{6,22},{7,5},{8,24},{9,11},... | collective-permute-start | bytes 7077896 | tf_op jit(solution)/shard_map/ppermute | solution.py:142
  471.6 39.1 %collective-permute-start.63 = (bf16[2,192,1152]{2,1,0:T(8,128)(2,1)S(1)}, bf16[2,192,1152]{2,1,0:T(8,128)(2,1)S(1)}, u32[]{:S(2)}, u32[]{:S(2)}) collective-permute-start(bf16[2,192,1152]{2,1,0:T(8,128)(2,1)S(1)} %pad_maximum_fusion.24), channel_id=1, source_target_pairs={{0,16},{1,17},{2,18},{3,19},{4,20},{5,21},{6,22},{7,23},{8,24},{9,... | collective-permute-start | bytes 2654216 | tf_op jit(solution)/shard_map/ppermute | solution.py:142
  510.7 67.3 %collective-permute-start.25 = (bf16[384,1536]{1,0:T(8,128)(2,1)}, bf16[384,1536]{1,0:T(8,128)(2,1)}, u32[]{:S(2)}, u32[]{:S(2)}) collective-permute-start(bf16[384,1536]{1,0:T(8,128)(2,1)} %get-tuple-element.61), channel_id=1, source_target_pairs={{0,1},{1,0},{2,3},{3,2},{4,5},{5,4},{6,7},{7,6},{8,9},{9,8},{10,11... | collective-permute-start | bytes 3538952 | tf_op jit(solution)/shard_map/ppermute | solution.py:142
  534.3 50.4 %collective-permute-start.50 = (bf16[2,2,96,768]{3,2,0,1:T(8,128)(2,1)}, bf16[2,2,96,768]{3,2,0,1:T(8,128)(2,1)}, u32[]{:S(2)}, u32[]{:S(2)}) collective-permute-start(bf16[2,2,96,768]{3,2,0,1:T(8,128)(2,1)} %bitcast.521), channel_id=1, source_target_pairs={{0,2},{1,3},{2,0},{3,1},{4,6},{5,7},{6,4},{7,5},{8,10},{9,11},{10,... | collective-permute-start | bytes 1769480 | tf_op jit(solution)/shard_map/ppermute | solution.py:142
  534.9 52.5 %collective-permute-start.52 = (bf16[2,2,96,768]{3,2,0,1:T(8,128)(2,1)}, bf16[2,2,96,768]{3,2,0,1:T(8,128)(2,1)}, u32[]{:S(2)}, u32[]{:S(2)}) collective-permute-start(bf16[2,2,96,768]{3,2,0,1:T(8,128)(2,1)} %bitcast.520), channel_id=1, source_target_pairs={{0,16},{1,17},{2,18},{3,19},{4,20},{5,21},{6,22},{7,23},{8,24},{9,... | collective-permute-start | bytes 1769480 | tf_op jit(solution)/shard_map/ppermute | solution.py:142
  567.2 78.6 %collective-permute-start.35 = (bf16[384,1536]{1,0:T(8,128)(2,1)S(1)}, bf16[384,1536]{1,0:T(8,128)(2,1)S(1)}, u32[]{:S(2)}, u32[]{:S(2)}) collective-permute-start(bf16[384,1536]{1,0:T(8,128)(2,1)S(1)} %fusion.61), channel_id=1, source_target_pairs={{0,1},{1,0},{2,3},{3,2},{4,5},{5,4},{6,7},{7,6},{8,9},{9,8},{10,11... | collective-permute-start | bytes 3538952 | tf_op jit(solution)/shard_map/ppermute | solution.py:142
  584.7 91.5 %collective-permute-start.59 = (bf16[2,192,1152]{2,1,0:T(8,128)(2,1)}, bf16[2,192,1152]{2,1,0:T(8,128)(2,1)}, u32[]{:S(2)}, u32[]{:S(2)}) collective-permute-start(bf16[2,192,1152]{2,1,0:T(8,128)(2,1)} %pad_maximum_fusion.22), channel_id=1, source_target_pairs={{0,16},{1,17},{2,18},{3,19},{4,20},{5,21},{6,22},{7,23},{8,24},{9,... | collective-permute-start | bytes 2654216 | tf_op jit(solution)/shard_map/ppermute | solution.py:142
  587.4 40.3 %collective-permute-start.51 = (bf16[2,96,768]{2,1,0:T(8,128)(2,1)S(1)}, bf16[2,96,768]{2,1,0:T(8,128)(2,1)S(1)}, u32[]{:S(2)}, u32[]{:S(2)}) collective-permute-start(bf16[2,96,768]{2,1,0:T(8,128)(2,1)S(1)} %dynamic-slice_bitcast_fusion.7), channel_id=1, source_target_pairs={{0,16},{1,17},{2,18},{3,19},{4,20},{5,21},{6,22},{7,23},{8,24},{9,... | collective-permute-start | bytes 884744 | tf_op jit(solution)/shard_map/ppermute | solution.py:142
  650.2 52.9 %collective-permute-start.36 = (bf16[384,1536]{1,0:T(8,128)(2,1)}, bf16[384,1536]{1,0:T(8,128)(2,1)}, u32[]{:S(2)}, u32[]{:S(2)}) collective-permute-start(bf16[384,1536]{1,0:T(8,128)(2,1)} %add_convert_fusion.1), channel_id=1, source_target_pairs={{0,1},{1,0},{2,3},{3,2},{4,5},{5,4},{6,7},{7,6},{8,9},{9,8},{10,11... | collective-permute-start | bytes 3538952 | tf_op jit(solution)/shard_map/ppermute | solution.py:142
  (128 other events, 1554.2 us)
Sparse Core Ops, SparseCore 0:
  62.5 128.1 all-gather.4
  192.3 68.1 all-gather.6
  334.0 69.7 reduce-scatter.7
  406.0 66.6 reduce-scatter.3
  474.9 66.6 reduce-scatter.5

commit v3 on v1

v3 whole, which is shorter than its diff:
```python
import math

import jax
import jax.numpy as jnp
from jax import lax
from jax.experimental import pallas as pl
from jax.experimental.pallas import tpu as pltpu
from jax.sharding import PartitionSpec as P

HD = 128
SEQ = 768
NSEG = 3


EPSILON = 1e-06
THETA = 10000.0
MASKED_SCORE = -1e30


def layout(lengths):
    segment_ends = jnp.cumsum(lengths, axis=-1)
    segment_starts = segment_ends - lengths
    places = jnp.arange(SEQ, dtype=jnp.int32)
    segment = jnp.sum((places[:, None] >= segment_ends[..., None, :]).astype(jnp.int32), axis=-1)
    choose = segment[..., None] == jnp.arange(NSEG, dtype=jnp.int32)
    picked = jnp.sum(jnp.where(choose, segment_starts[..., None, :], 0), axis=-1)
    return (segment, places - picked)


def angles(position):
    frequency = jnp.exp(-(math.log(THETA) * 2.0 / HD) * jnp.arange(HD // 2, dtype=jnp.float32))
    phase_angle = position.astype(jnp.float32)[..., None] * frequency
    phase_angle = jnp.concatenate([phase_angle, phase_angle], axis=-1)
    return (jnp.cos(phase_angle), jnp.sin(phase_angle))


def plain_dot(left_side, right_side):
    return jnp.dot(left_side, right_side, preferred_element_type=jnp.float32)


def trans_dot(left_side, right_side):
    return lax.dot_general(
        left_side, right_side, (((1,), (1,)), ((), ())), preferred_element_type=jnp.float32
    )


def outer_dot(left_side, right_side):
    return lax.dot_general(
        left_side, right_side, (((0,), (0,)), ((), ())), preferred_element_type=jnp.float32
    )


BLOCK = 256


def rotated(values, cosine, signed_sine):
    return values * cosine + pltpu.roll(values, HD // 2, 1) * signed_sine


def unrotated(values, cosine, signed_sine):
    return values * cosine - pltpu.roll(values, HD // 2, 1) * signed_sine


def allowed_block(start, top, width):
    row = top + lax.broadcasted_iota(jnp.int32, (BLOCK, width), 0)
    col = lax.broadcasted_iota(jnp.int32, (BLOCK, width), 1)
    return (col >= start) & (col <= row)


def attend_body(
    q_pre, k_pre, v_pre, cosine, signed_sine, start, q_out, k_out, v_out, att_out, lse_out
):
    head = pl.program_id(0)

    @pl.when(head == 0)
    def _():
        k_out[...] = rotated(k_pre[...], cosine[...], signed_sine[...]).astype(jnp.bfloat16)
        v_out[...] = v_pre[...].astype(jnp.bfloat16)
        lse_out[...] = jnp.zeros_like(lse_out)

    q_out[...] = rotated(q_pre[...], cosine[...], signed_sine[...]).astype(jnp.bfloat16)
    for top in range(0, SEQ, BLOCK):
        width = top + BLOCK
        rows = pl.ds(top, BLOCK)
        scores = trans_dot(q_out[rows, :], k_out[:width, :]) * HD ** (-0.5)
        scores = jnp.where(allowed_block(start[rows, :], top, width), scores, MASKED_SCORE)
        row_max = jnp.max(scores, axis=1, keepdims=True)
        terms = jnp.exp(scores - row_max)
        total = jnp.sum(terms, axis=1, keepdims=True)
        probs = (terms * (1.0 / total)).astype(jnp.bfloat16)
        att_out[rows, :] = plain_dot(probs, v_out[:width, :]).astype(jnp.bfloat16)
        lane = lax.broadcasted_iota(jnp.int32, (BLOCK, HD), 1)
        lse_out[rows, :] = jnp.where(lane == head, row_max + jnp.log(total), lse_out[rows, :])


def attend_back_body(
    q_rot, k_rot, v_low, d_att, lse, cosine, signed_sine, start, grad_out, dk_sum, dv_sum
):
    head = pl.program_id(0)

    @pl.when(head == 0)
    def _():
        dk_sum[...] = jnp.zeros_like(dk_sum)
        dv_sum[...] = jnp.zeros_like(dv_sum)

    for top in range(0, SEQ, BLOCK):
        width = top + BLOCK
        rows = pl.ds(top, BLOCK)
        query = q_rot[rows, :]
        d_out = d_att[rows, :]
        lane = lax.broadcasted_iota(jnp.int32, (BLOCK, HD), 1)
        row_lse = jnp.sum(jnp.where(lane == head, lse[rows, :], 0.0), axis=1, keepdims=True)
        scores = trans_dot(query, k_rot[:width, :]) * HD ** (-0.5)
        scores = jnp.where(allowed_block(start[rows, :], top, width), scores, MASKED_SCORE)
        probs = jnp.exp(scores - row_lse)
        d_probs = trans_dot(d_out, v_low[:width, :])
        inner = jnp.sum(probs * d_probs, axis=1, keepdims=True)
        d_scores = (probs * (d_probs - inner)).astype(jnp.bfloat16)
        d_query = plain_dot(d_scores, k_rot[:width, :]) * HD ** (-0.5)
        d_query = unrotated(d_query, cosine[rows, :], signed_sine[rows, :])
        cols = pl.ds(pl.multiple_of(head * HD, HD), HD)
        grad_out[rows, cols] = d_query.astype(jnp.bfloat16)
        dk_sum[:width, :] += outer_dot(d_scores, query)
        dv_sum[:width, :] += outer_dot(probs.astype(jnp.bfloat16), d_out)

    @pl.when(head == pl.num_programs(0) - 1)
    def _():
        edge = grad_out.shape[1] - 2 * HD
        d_key = unrotated(dk_sum[...] * HD ** (-0.5), cosine[...], signed_sine[...])
        grad_out[:, edge : edge + HD] = d_key.astype(jnp.bfloat16)
        grad_out[:, edge + HD :] = dv_sum[...].astype(jnp.bfloat16)


def fixed(shape):
    return pl.BlockSpec(shape, lambda head: (0, 0))


def column(index):
    return pl.BlockSpec((SEQ, HD), lambda head: (0, index))


PER_HEAD = pl.BlockSpec((SEQ, HD), lambda head: (0, head))
WHOLE = (SEQ, HD)


def attend(qkv_pre, cosine, signed_sine, start):
    heads = qkv_pre.shape[1] // HD - 2
    shape = lambda cols, kind: jax.ShapeDtypeStruct((SEQ, cols), kind)
    low = jnp.bfloat16
    return pl.pallas_call(
        attend_body,
        grid=(heads,),
        in_specs=[PER_HEAD, column(heads), column(heads + 1)]
        + [fixed(WHOLE), fixed(WHOLE), fixed((SEQ, 1))],
        out_specs=[PER_HEAD, fixed(WHOLE), fixed(WHOLE), PER_HEAD, fixed(WHOLE)],
        out_shape=[
            shape(heads * HD, low),
            shape(HD, low),
            shape(HD, low),
            shape(heads * HD, low),
            shape(HD, jnp.float32),
        ],
    )(qkv_pre, qkv_pre, qkv_pre, cosine, signed_sine, start)


def attend_back(q_rot, k_rot, v_low, d_att, lse, cosine, signed_sine, start):
    heads = q_rot.shape[1] // HD
    cols = (heads + 2) * HD
    return pl.pallas_call(
        attend_back_body,
        grid=(heads,),
        in_specs=[PER_HEAD, fixed(WHOLE), fixed(WHOLE), PER_HEAD, fixed(WHOLE)]
        + [fixed(WHOLE), fixed(WHOLE), fixed((SEQ, 1))],
        out_specs=fixed((SEQ, cols)),
        out_shape=jax.ShapeDtypeStruct((SEQ, cols), jnp.bfloat16),
        scratch_shapes=[pltpu.VMEM(WHOLE, jnp.float32), pltpu.VMEM(WHOLE, jnp.float32)],
    )(q_rot, k_rot, v_low, d_att, lse, cosine, signed_sine, start)


AXES = ("group", "dp", "tensor")


def routes(dp_count):
    def table(move):
        flat = lambda g, d, t: (g * dp_count + d) * 2 + t
        return [
            (flat(g, d, t), flat(*move(g, d, t)))
            for g in range(2)
            for d in range(dp_count)
            for t in range(2)
        ]

    shifts = {
        step: table(lambda g, d, t: (g, (d + 2 * step) % dp_count, t))
        for step in range(1, dp_count // 2)
    }
    return shifts | {
        "x": table(lambda g, d, t: (g, d ^ 1, t)),
        "y": table(lambda g, d, t: (g ^ 1, d, t)),
        "t": table(lambda g, d, t: (g, d, t ^ 1)),
        "first": table(lambda g, d, t: (g, d ^ 1, t) if t == 0 else (g ^ 1, d, t)),
        "second": table(lambda g, d, t: (g ^ 1, d, t) if t == 0 else (g, d ^ 1, t)),
    }


def local(
    inputs,
    cotangent,
    lengths,
    attn_gain,
    w_query,
    b_query,
    w_key,
    b_key,
    w_value,
    b_value,
    w_out,
    ffn_gain,
    w_gate,
    w_up,
    w_down,
):
    bf16 = jnp.bfloat16
    f32 = jnp.float32
    dp_count = lax.axis_size("dp")
    line = dp_count // 2
    dp_index = lax.axis_index("dp")
    x_index = dp_index % 2
    z_index = dp_index // 2
    y_index = lax.axis_index("group")
    core = lax.axis_index("tensor")
    table = routes(dp_count)
    line_groups = [[2 * z + x for z in range(line)] for x in range(2)]
    tokens, d_model = inputs.shape
    half = tokens // 2
    rows = w_query.shape[0]
    head_count = w_query.shape[1] // HD
    kv_count = w_key.shape[1] // HD
    ffn_cols = w_gate.shape[1]
    quarter = -(-ffn_cols // 512) * 128

    def send(value, route):
        return lax.ppermute(value, AXES, table[route])

    def pick(value, index):
        return lax.dynamic_index_in_dim(value, index, 0, keepdims=False)

    def in_order(index, mine, other):
        first = index == 0
        return jnp.where(first, mine, other), jnp.where(first, other, mine)

    def my_half(value):
        return pick(value.reshape(2, half, value.shape[-1]), core)

    def other_half(value):
        return pick(value.reshape(2, half, value.shape[-1]), 1 - core)

    def both_halves(mine):
        return jnp.concatenate(in_order(core, mine, send(mine, "t")), axis=0)

    def after(value, *others):
        return lax.optimization_barrier((value, *others))[0]

    def square_far(mine, near, *others):
        mine_sib = send(mine, "t")
        near_sib = send(near, "t")
        far = send(after(jnp.stack([mine, near]), *others), "second")
        far_sib = send(far, "t")
        whole = jnp.concatenate(
            [mine, near, far[0], far[1], mine_sib, near_sib, far_sib[0], far_sib[1]], axis=0
        )
        return whole, far

    def square_scatter(mine, theirs, *others):
        came = send(theirs, "t")
        total = (mine.astype(f32) + came.astype(f32)).reshape(4, half, d_model)
        came = send(after(total[2:].astype(bf16), *others), "second")
        total = total[:2] + came.astype(f32)
        came = send(total[1].astype(bf16), "first")
        return total[0] + came.astype(f32)

    def ffn_quarter(weight, index):
        parts = [weight[:, i * quarter : (i + 1) * quarter] for i in range(4)]
        parts[3] = jnp.pad(parts[3], ((0, 0), (0, 4 * quarter - ffn_cols)))
        upper = jnp.where(index % 2 == 0, parts[2], parts[3])
        lower = jnp.where(index % 2 == 0, parts[0], parts[1])
        return jnp.where(index < 2, lower, upper)

    def ffn_pair(weights):
        other = [ffn_quarter(w, (1 - x_index) * 2 + y_index) for w in weights]
        came = send(jnp.concatenate(other, axis=1), "x")
        mine = [ffn_quarter(w, x_index * 2 + y_index) for w in weights]
        return jnp.stack(in_order(x_index, jnp.concatenate(mine, axis=1), came))

    def ffn_gather(pair):
        full = lax.all_gather(pair, "dp", axis=0, axis_index_groups=line_groups)
        return full.reshape(d_model, pair.shape[-1])

    def ffn_scatter(grad):
        parts = grad.astype(bf16).reshape(line, 2 * rows, quarter)
        return lax.psum_scatter(
            parts, "dp", scatter_dimension=0, axis_index_groups=line_groups
        ).reshape(2, rows, quarter)

    def ffn_swap(summed):
        came = send(pick(summed, 1 - x_index), "x")
        pair = jnp.stack(in_order(x_index, pick(summed, x_index), came))
        low, high = in_order(y_index, pair, send(pair, "y"))
        whole = jnp.concatenate([low[0], high[0], low[1], high[1]], axis=1)
        return whole[:, :ffn_cols].astype(f32)

    cut = line // 2
    part_rows = rows // 2

    def line_sends(weight):
        mine = lax.dynamic_slice_in_dim(weight, y_index * part_rows, part_rows, 0)
        return [mine] + [send(mine, step) for step in range(1, line)]

    def line_join(pieces):
        whole = jnp.zeros((line,) + pieces[0].shape, bf16)
        for step, piece in enumerate(pieces):
            spot = ((z_index - step) % line, 0, 0)
            whole = lax.dynamic_update_slice(whole, piece[None], spot)
        return whole

    def near_sends(blocks):
        low, high = blocks[:cut], blocks[cut:]
        return low, high, send(low, "x"), send(high, "y")

    def far_join(low, high, low_near, high_near):
        low_far = send(jnp.stack([low, low_near]), "y")
        high_far = send(jnp.stack([high, high_near]), "x")
        cols = low.shape[-1]
        whole = jnp.zeros((line, 2, 2, part_rows, cols), bf16)
        x, y = x_index, y_index
        for piece, z, px, py in (
            (low, 0, x, y),
            (low_near, 0, 1 - x, y),
            (low_far[0], 0, x, 1 - y),
            (low_far[1], 0, 1 - x, 1 - y),
            (high, cut, x, y),
            (high_near, cut, x, 1 - y),
            (high_far[0], cut, 1 - x, y),
            (high_far[1], cut, 1 - x, 1 - y),
        ):
            whole = lax.dynamic_update_slice(whole, piece[:, None, None], (z, px, py, 0, 0))
        return whole.reshape(d_model, cols)

    def take(value, axis, index):
        return lax.dynamic_index_in_dim(value, index, axis, keepdims=False)

    def fold(value, axis, index, route):
        came = send(take(value, axis, 1 - index), route)
        return (take(value, axis, index).astype(f32) + came.astype(f32)).astype(bf16)

    def attn_scatter(grad):
        view = grad.reshape(line, 2, 2, part_rows, grad.shape[-1])
        low = fold(view[:cut], 1, x_index, "x")
        high = fold(view[cut:], 2, y_index, "y")
        low = fold(low, 1, y_index, "y")
        high = fold(high, 1, x_index, "x")
        blocks = jnp.concatenate([low, high])
        total = pick(blocks, z_index).astype(f32)
        for step in range(1, line):
            total = total + send(pick(blocks, (z_index + step) % line), step).astype(f32)
        mine = total.astype(bf16)
        whole = jnp.concatenate(in_order(y_index, mine, send(mine, "y"))).astype(f32)
        return whole, blocks, mine

    query_cols = head_count * HD
    key_cols = kv_count * HD
    qkv_cols = query_cols + 2 * key_cols
    gains = jnp.pad(jnp.stack([attn_gain, ffn_gain], axis=1), ((0, 0), (0, HD - 2)))

    qkv_pieces = line_sends(jnp.concatenate([w_query, w_key, w_value, gains], axis=1))
    gate_up_pair = ffn_pair([w_gate, w_up])
    gate_up_full = ffn_gather(gate_up_pair)
    out_pieces = line_sends(after(w_out, *qkv_pieces))
    qkv_near = near_sends(line_join(qkv_pieces))
    qkv_full = far_join(*qkv_near)
    out_near = near_sends(after(line_join(out_pieces), *qkv_near))
    out_full = far_join(*out_near)
    cot_half = my_half(cotangent)
    cot_near = send(after(cot_half, *out_near), "first")
    down_pair = ffn_pair([after(w_down, *out_near)])

    segment, position = layout(lengths[0])
    cosine, sine_table = angles(position)
    sign = jnp.where(jnp.arange(HD) < HD // 2, -1.0, 1.0)
    signed_sine = sine_table * sign
    start = (jnp.arange(SEQ, dtype=jnp.int32) - position)[:, None]
    stream = inputs.astype(f32)
    inv_one = lax.rsqrt(jnp.mean(stream * stream, axis=-1, keepdims=True) + EPSILON)
    qkv_full = after(qkv_full, cosine, signed_sine, start, inv_one)
    gain_one = qkv_full[:, qkv_cols].astype(f32)
    gain_two = qkv_full[:, qkv_cols + 1].astype(f32)
    qkv_full = qkv_full[:, :qkv_cols]

    h_one = (stream * inv_one * gain_one).astype(bf16)
    qkv_bias = jnp.concatenate([b_query, b_key, b_value]).astype(f32)
    qkv_pre = plain_dot(h_one, qkv_full) + qkv_bias
    q_rot, k_rot, v_low, attended, lse = attend(qkv_pre, cosine, signed_sine, start)
    branch = trans_dot(attended, out_full)
    resid = (
        my_half(stream)
        + my_half(branch)
        + send(other_half(branch).astype(bf16), "t").astype(f32)
    )
    inv_two = lax.rsqrt(jnp.mean(resid * resid, axis=-1, keepdims=True) + EPSILON)
    norm_two = resid * inv_two
    h_two_half = after((norm_two * gain_two).astype(bf16), down_pair)
    h_two, h_two_far = square_far(h_two_half, send(h_two_half, "first"))
    cot_all, _ = square_far(cot_half, cot_near, h_two_far)
    down_full = ffn_gather(after(down_pair, gate_up_pair))

    gate_full = gate_up_full[:, :quarter]
    up_full = gate_up_full[:, quarter:]
    gate_low = plain_dot(h_two, gate_full).astype(bf16)
    up_low = plain_dot(h_two, up_full).astype(bf16)
    gate_pre = gate_low.astype(f32)
    up_pre = up_low.astype(f32)
    sigmoid_gate = jax.nn.sigmoid(gate_pre)
    swish_gate = gate_pre * sigmoid_gate
    hidden = (swish_gate * up_pre).astype(bf16)
    down_part = outer_dot(cot_all, hidden).astype(bf16)
    down_sum = ffn_scatter(down_part)
    d_hidden = plain_dot(after(cot_all, down_part), down_full)
    d_gate = (d_hidden * up_pre * sigmoid_gate * (1.0 + gate_pre * (1.0 - sigmoid_gate))).astype(
        bf16
    )
    d_up = (d_hidden * swish_gate).astype(bf16)
    mid = 4 * half

    def entry(gate_side, up_side):
        return (trans_dot(gate_side, gate_full) + trans_dot(up_side, up_full)).astype(bf16)

    theirs = entry(d_gate[mid:], d_up[mid:])
    mine = entry(after(d_gate[:mid], theirs), d_up[:mid])
    d_h_two = square_scatter(mine, theirs)
    gate_part = outer_dot(after(h_two, mine), d_gate).astype(bf16)
    gate_sum = ffn_scatter(gate_part)
    up_part = outer_dot(after(h_two, gate_part), d_up).astype(bf16)
    up_sum = ffn_scatter(up_part)
    low_hidden = after(hidden, up_part)
    ffn_theirs = trans_dot(low_hidden[mid:], down_full).astype(bf16)
    ffn_mine = trans_dot(low_hidden[:mid], down_full).astype(bf16)

    scaled = d_h_two * gain_two
    d_resid = cot_half.astype(f32) + inv_two * (
        scaled - norm_two * jnp.mean(norm_two * scaled, axis=-1, keepdims=True)
    )
    gain_two_part = jnp.sum(d_h_two * norm_two, axis=0)
    d_out_low = both_halves(d_resid.astype(bf16))
    out_grad, _, _ = attn_scatter(outer_dot(d_out_low, attended).astype(bf16))
    ffn_total = square_scatter(ffn_mine, ffn_theirs, d_out_low)
    layer_out = both_halves((resid + ffn_total).astype(bf16))
    d_attended = plain_dot(d_out_low, out_full).astype(bf16)
    d_qkv = attend_back(q_rot, k_rot, v_low, d_attended, lse, cosine, signed_sine, start)
    qkv_grad, qkv_blocks, qkv_mine = attn_scatter(outer_dot(h_one, d_qkv).astype(bf16))
    down_grad = ffn_swap(after(down_sum, d_out_low))
    gate_grad = ffn_swap(after(gate_sum, qkv_blocks))
    up_grad = ffn_swap(after(up_sum, qkv_mine))
    entry_one = trans_dot(d_qkv, qkv_full)
    d_h_one = my_half(entry_one) + send(other_half(entry_one).astype(bf16), "t").astype(f32)
    half_inv = my_half(inv_one)
    norm_one = my_half(stream) * half_inv
    scaled = d_h_one * gain_one
    input_grad = both_halves(
        (
            d_resid
            + half_inv * (scaled - norm_one * jnp.mean(norm_one * scaled, axis=-1, keepdims=True))
        ).astype(bf16)
    )
    gain_one_part = jnp.sum(d_h_one * norm_one, axis=0)

    bias_part = jnp.sum(d_qkv.astype(f32), axis=0)
    small = jnp.concatenate([gain_one_part, gain_two_part, bias_part]).reshape(-1, 128)
    small = small + send(small, "y")
    step = 1
    while step < dp_count:
        small = small + lax.ppermute(small, "dp", [(i, i ^ step) for i in range(dp_count)])
        step *= 2
    small = small.reshape(-1)
    gain_sums = small[: 2 * d_model].reshape(2, dp_count, rows)
    gain_mine = lax.dynamic_index_in_dim(gain_sums, dp_index, 1, keepdims=False)
    gain_mine = gain_mine + send(gain_mine, "t")
    bias_sum = small[2 * d_model :]
    return (
        layer_out,
        input_grad,
        gain_mine[0],
        qkv_grad[:, :query_cols],
        bias_sum[:query_cols],
        qkv_grad[:, query_cols : query_cols + key_cols],
        bias_sum[query_cols : query_cols + key_cols],
        qkv_grad[:, query_cols + key_cols :],
        bias_sum[query_cols + key_cols :],
        out_grad,
        gain_mine[1],
        gate_grad,
        up_grad,
        down_grad,
    )


def solution(mesh):
    in_specs = (
        P(("group", "dp"), None),
        P(("group", "dp"), None),
        P(("group", "dp"), None),
        P("dp"),
        P("dp", "tensor"),
        P("tensor"),
        P("dp", "tensor"),
        P("tensor"),
        P("dp", "tensor"),
        P("tensor"),
        P("dp", "tensor"),
        P("dp"),
        P("dp", "tensor"),
        P("dp", "tensor"),
        P("dp", "tensor"),
    )
    out_specs = (
        P(("group", "dp"), None),
        P(("group", "dp"), None),
        P("dp"),
        P("dp", "tensor"),
        P("tensor"),
        P("dp", "tensor"),
        P("tensor"),
        P("dp", "tensor"),
        P("tensor"),
        P("dp", "tensor"),
        P("dp"),
        P("dp", "tensor"),
        P("dp", "tensor"),
        P("dp", "tensor"),
    )
    return jax.shard_map(local, mesh=mesh, in_specs=in_specs, out_specs=out_specs, check_vma=False)
```

time: 877 us -> 728 us (0.83)
  waiting for transfers between devices: 384 us -> 246 us
  Pallas kernels: 0 us -> 29.9 us
  matrix products: 240 us -> 212 us
  local copies, waits for them, and re-layouts: 87.7 us -> 77.3 us
    ppermute x34 -> x61, waiting for transfers between devices: 114 us -> 237 us  [send(): return lax.ppermute(value, AXES, table[route])]
    reduce_scatter x3, waiting for transfers between devices: 88.7 us -> 0.01 us  [ffn_scatter(): lax.psum_scatter(parts, 'dp', scatter_dimension=0, axis_index_groups=line...]
    all_gather x3 -> x2, waiting for transfers between devices: 77.1 us -> 0.01 us  [ffn_gather(): full = lax.all_gather(pair, 'dp', axis=0, axis_index_groups=line_groups)]
    reduce_scatter x2 -> x0, waiting for transfers between devices: 66.6 us -> none  [attn_scatter(): lax.psum_scatter(grad.astype(bf16), 'dp', scatter_dimension=0, tiled=True)]
    all_gather x2 -> x0, waiting for transfers between devices: 33.1 us -> none  [the longest x1 22.2 us: local(): lax.all_gather(jnp.concatenate([w_query, w_key, w_value, gains], axis=1),...]
    dot_general x6 -> x0, matrix products: 30.9 us -> none  [the longest x1 12 us: local(): jnp.einsum('qkgd,skd->kgqs', d_attended, values_low, preferred_element_ty...]
    pallas_call x0 -> x2, Pallas kernels: none -> 29.9 us  [the longest x1 16.9 us: attend_back(): pl.pallas_call(attend_back_body, grid=(heads,), in_specs=[PER_HEAD, fixed...]
    dynamic_update_slice x0 -> x23, local copies, waits for them, and re-layouts: none -> 24.2 us  [the longest x16 20.3 us: far_join(): lax.dynamic_update_slice(whole, piece[:, None, None], (z, px, py, 0, 0))]
  transfers between devices with their start and end apart: 47 -> 69, of which waited for: 21 -> 29; matrix products, arithmetic and copies ran while one was open for 38% -> 41% of each run, Pallas kernels for 0% -> 4%
where the time goes in v3:
time: 728 us; the launch traced here: 719 us
  waiting for transfers between devices  246 us (34%)
  matrix products  212 us (29%)
  local copies, waits for them, and re-layouts  77.3 us (11%)
  starting transfers between devices  71.3 us (10%)
  other arithmetic  65.9 us (9%)
  Pallas kernels  29.9 us (4%)
  between operations  15.7 us (2%)
    ppermute x61, waiting for transfers between devices, send(): return lax.ppermute(value, AXES, table[route])  237 us
    dot_general x5, matrix products, plain_dot(): return jnp.dot(left_side, right_side, preferred_element_type=jnp.float32)  74.6 us
    dot_general x8, matrix products, trans_dot(): lax.dot_general(left_side, right_side, (((1,), (1,)), ((), ())), preferre...  73.1 us
    ppermute x61, starting transfers between devices, send(): return lax.ppermute(value, AXES, table[route])  65.5 us
    dot_general x5, matrix products, outer_dot(): lax.dot_general(left_side, right_side, (((0,), (0,)), ((), ())), preferre...  64.4 us
    dynamic_update_slice x16, local copies, waits for them, and re-layouts, far_join(): lax.dynamic_update_slice(whole, piece[:, None, None], (z, px, py, 0, 0))  20.3 us
    unnamed x144, local copies, waits for them, and re-layouts  19.8 us
    pallas_call x1, Pallas kernels, attend_back(): pl.pallas_call(attend_back_body, grid=(heads,), in_specs=[PER_HEAD, fixed...  16.9 us
  transfers between devices with their start and end apart: 69, of which 29 were waited for; matrix products, arithmetic and copies ran while one was open for 41% of the time, Pallas kernels for 4%

profile of v3, /device:TPU:0, one launch (start us, length us, event | category | flops | bytes accessed | tf_op | source)
XLA Modules:
  0.0 718.6 jit_solution(2636522979434671171)
XLA Ops:
  73.5 13.6 %collective-permute-done.12 = bf16[2,96,768]{2,1,0:T(8,128)(2,1)} collective-permute-done((bf16[2,96,768]{2,1,0:T(8,128)(2,1)}, bf16[2,96,768]{2,1,0:T(8,128)(2,1)}, u32[]{:S(2)}, u32[]{:S(2)}) %collective-permute-start.12) | collective-permute-done | bytes 294944 | tf_op jit(solution)/shard_map/ppermute | solution.py:243
  118.2 13.0 %shard_map.254 = (bf16[768,768]{1,0:T(8,128)(2,1)}, bf16[768,128]{1,0:T(8,128)(2,1)}, bf16[768,128]{1,0:T(8,128)(2,1)}, bf16[768,768]{1,0:T(8,128)(2,1)}, f32[768,128]{1,0:T(8,128)}) custom-call(f32[768,1024]{1,0:T(8,128)} %fusion.33.q_pre.k_pre.v_pre, f32[768,1024]{1,0:T(8,128)} %fusion.33.q_pre.k_pre.v_pre, f32[768,1024]{1,0:T(8,128)} %fusion.33.q_pre.k_pre.v_pre, ...), custom_call_target="tpu_custom_call" | custom-call | tf_op jit(solution)/shard_map/pallas_call | solution.py:150
  151.1 14.7 %collective-permute-done.16 = bf16[384,1536]{1,0:T(8,128)(2,1)S(1)} collective-permute-done((bf16[384,1536]{1,0:T(8,128)(2,1)S(1)}, bf16[384,1536]{1,0:T(8,128)(2,1)S(1)}, u32[]{:S(2)}, u32[]{:S(2)}) %collective-permute-start.16) | collective-permute-done | bytes 1179680 | tf_op jit(solution)/shard_map/ppermute | solution.py:243
  170.9 27.3 %collective-permute-done.22 = bf16[384,1536]{1,0:T(8,128)(2,1)S(1)} collective-permute-done((bf16[384,1536]{1,0:T(8,128)(2,1)S(1)}, bf16[384,1536]{1,0:T(8,128)(2,1)S(1)}, u32[]{:S(2)}, u32[]{:S(2)}) %collective-permute-start.22) | collective-permute-done | bytes 1179680 | tf_op jit(solution)/shard_map/ppermute | solution.py:243
  214.2 22.5 %collective-permute-done.23 = bf16[2,384,1536]{2,1,0:T(8,128)(2,1)S(1)} collective-permute-done((bf16[2,384,1536]{2,1,0:T(8,128)(2,1)S(1)}, bf16[2,384,1536]{2,1,0:T(8,128)(2,1)S(1)}, u32[]{:S(2)}, u32[]{:S(2)}) %collective-permute-start.23) | collective-permute-done | bytes 2359328 | tf_op jit(solution)/shard_map/ppermute | solution.py:243
  248.6 18.1 %convolution_convert_fusion.1 = bf16[3072,1152]{1,0:T(8,128)(2,1)} fusion(bf16[3072,1536]{1,0:T(8,128)(2,1)} %copy-done.39, bf16[1536,2304]{1,0:T(8,128)(2,1)} %bitcast.441), kind=kOutput, calls=%fused_computation.15 | convolution fusion | flops 10875174912 | bytes 20054016 | tf_op jit(solution)/shard_map/dot_general | solution.py:38
  266.7 18.3 %fusion = (bf16[3072,1152]{1,0:T(8,128)(2,1)}, bf16[3072,1152]{1,0:T(8,128)(2,1)}) fusion(bf16[3072,1152]{1,0:T(8,128)(2,1)} %convolution_convert_fusion.1, bf16[3072,1536]{1,0:T(8,128)(2,1)S(1)} %bitcast.436, bf16[1536,2304]{1,0:T(8,128)(2,1)} %bitcast.442), kind=kOutput, calls=%fused_computation.5 | convolution fusion | flops 10903486464 | bytes 34209792 | tf_op jit(solution)/shard_map/dot_general | solution.py:38
  285.1 17.9 %convolution_convert_fusion.6 = bf16[1536,1152]{1,0:T(8,128)(2,1)} fusion(bf16[3072,1536]{1,0:T(8,128)(2,1)} %fusion.42, bf16[3072,1152]{1,0:T(8,128)(2,1)} %get-tuple-element.49), kind=kOutput, calls=%fused_computation.24 | convolution fusion | flops 10873405440 | bytes 20054016 | tf_op jit(solution)/shard_map/dot_general | solution.py:48
  303.0 26.4 %multiply_convert_fusion = (bf16[3072,1152]{1,0:T(8,128)(2,1)}, bf16[3072,1152]{1,0:T(8,128)(2,1)}) fusion(bf16[3072,1152]{1,0:T(8,128)(2,1)} %convolution_convert_fusion.1, bf16[3072,1152]{1,0:T(8,128)(2,1)} %get-tuple-element.153, bf16[3072,1536]{1,0:T(8,128)(2,1)} %fusion.42, bf16[1536,1152]{1,0:T(8,128)(2,1)} %bitcast.447), kind=kOutput, calls=%fused_computation.13 | convolution fusion | flops 10924720128 | bytes 41287680 | tf_op jit(solution)/shard_map/dot_general | solution.py:38
  329.4 9.7 %fusion.10 = f32[1536,1536]{1,0:T(8,128)S(1)} fusion(bf16[3072,1152]{1,0:T(8,128)(2,1)} %get-tuple-element.77, bf16[1536,2304]{1,0:T(8,128)(2,1)} %bitcast.443), kind=kOutput, calls=%fused_computation.34 | convolution fusion | flops 5435817984 | bytes 16515072 | tf_op jit(solution)/shard_map/dot_general | solution.py:42
  339.1 10.4 %add_convert_fusion.1 = bf16[1536,1536]{1,0:T(8,128)(2,1)} fusion(f32[1536,1536]{1,0:T(8,128)S(1)} %fusion.10, bf16[3072,1152]{1,0:T(8,128)(2,1)S(1)} %copy-done.56, bf16[1536,2304]{1,0:T(8,128)(2,1)} %bitcast.444), kind=kOutput, calls=%fused_computation.19 | convolution fusion | flops 5440536576 | bytes 21233664 | tf_op jit(solution)/shard_map/dot_general | solution.py:42
  352.4 10.9 %fusion.21 = f32[1536,1536]{1,0:T(8,128)} fusion(bf16[1536,1152]{1,0:T(8,128)(2,1)S(1)} %slice.396, bf16[1536,2304]{1,0:T(8,128)(2,1)} %bitcast.445), kind=kOutput, calls=%fused_computation.47 | convolution fusion | flops 5435817984 | bytes 16515072 | tf_op jit(solution)/shard_map/dot_general | solution.py:42
  363.2 12.7 %convert_add_fusion = f32[1536,1536]{1,0:T(8,128)S(1)} fusion(bf16[1536,1536]{1,0:T(8,128)(2,1)} %collective-permute-done.28, f32[1536,1536]{1,0:T(8,128)} %fusion.21, bf16[1536,2304]{1,0:T(8,128)(2,1)} %bitcast.446, bf16[3072,1152]{1,0:T(8,128)(2,1)} %get-tuple-element.76), kind=kOutput, calls=%fused_computation.16 | convolution fusion | flops 5447614464 | bytes 30670848 | tf_op jit(solution)/shard_map/dot_general | solution.py:42
  377.3 20.1 %convolution_convert_fusion.5 = bf16[1536,1152]{1,0:T(8,128)(2,1)} fusion(bf16[3072,1536]{1,0:T(8,128)(2,1)} %copy-done.39, bf16[3072,1152]{1,0:T(8,128)(2,1)} %get-tuple-element.77), kind=kOutput, calls=%fused_computation.23 | convolution fusion | flops 10873405440 | bytes 20054016 | tf_op jit(solution)/shard_map/dot_general | solution.py:48
  397.5 18.3 %convolution_convert_fusion.4 = bf16[1536,1152]{1,0:T(8,128)(2,1)} fusion(bf16[3072,1536]{1,0:T(8,128)(2,1)} %copy-done.39, bf16[3072,1152]{1,0:T(8,128)(2,1)} %get-tuple-element.76), kind=kOutput, calls=%fused_computation.22 | convolution fusion | flops 10873405440 | bytes 20054016 | tf_op jit(solution)/shard_map/dot_general | solution.py:48
  419.5 10.0 %convolution_convert_fusion.2 = bf16[1536,1536]{1,0:T(8,128)(2,1)} fusion(bf16[1536,1152]{1,0:T(8,128)(2,1)S(1)} %bitcast.448, bf16[3072,1152]{1,0:T(8,128)(2,1)} %get-tuple-element.49), kind=kOutput, calls=%fused_computation.20 | convolution fusion | flops 5438177280 | bytes 11796480 | tf_op jit(solution)/shard_map/dot_general | solution.py:42
  448.0 16.9 %shard_map.255 = bf16[768,1024]{1,0:T(8,128)(2,1)} custom-call(bf16[768,768]{1,0:T(8,128)(2,1)} %get-tuple-element.51.q_rot, bf16[768,128]{1,0:T(8,128)(2,1)} %get-tuple-element.52.k_rot, bf16[768,128]{1,0:T(8,128)(2,1)} %get-tuple-element.53.v_low, bf16[768,768]{1,0:T(8,128)(2,1)} %convolution_convert_fusion.9.d_att, f32[768,128]{1,0:T(8,128)} %get-tuple-element.54.lse, ...), custom_call_target="tpu_custom_call" | custom-call | tf_op jit(solution)/shard_map/pallas_call | solution.py:169
  477.7 10.7 %convert_add_fusion.1 = f32[1536,1536]{1,0:T(8,128)S(1)} fusion(bf16[1536,1536]{1,0:T(8,128)(2,1)} %collective-permute-done.27, bf16[1536,1152]{1,0:T(8,128)(2,1)S(1)} %bitcast.449, bf16[3072,1152]{1,0:T(8,128)(2,1)} %get-tuple-element.49), kind=kOutput, calls=%fused_computation.17 | convolution fusion | flops 5445255168 | bytes 21233664 | tf_op jit(solution)/shard_map/dot_general | solution.py:42
  511.9 10.7 %collective-permute-done.50 = bf16[2,2,96,768]{3,2,0,1:T(8,128)(2,1)S(1)} collective-permute-done((bf16[2,2,96,768]{3,2,0,1:T(8,128)(2,1)S(1)}, bf16[2,2,96,768]{3,2,0,1:T(8,128)(2,1)S(1)}, u32[]{:S(2)}, u32[]{:S(2)}) %collective-permute-start.50) | collective-permute-done | bytes 589856 | tf_op jit(solution)/shard_map/ppermute | solution.py:243
  525.2 14.4 %collective-permute-done.42 = bf16[2,2,96,1024]{3,2,0,1:T(8,128)(2,1)S(1)} collective-permute-done((bf16[2,2,96,1024]{3,2,0,1:T(8,128)(2,1)S(1)}, bf16[2,2,96,1024]{3,2,0,1:T(8,128)(2,1)S(1)}, u32[]{:S(2)}, u32[]{:S(2)}) %collective-permute-start.42) | collective-permute-done | bytes 786464 | tf_op jit(solution)/shard_map/ppermute | solution.py:243
  541.0 23.6 %collective-permute-done.51 = bf16[2,96,768]{2,1,0:T(8,128)(2,1)S(1)} collective-permute-done((bf16[2,96,768]{2,1,0:T(8,128)(2,1)S(1)}, bf16[2,96,768]{2,1,0:T(8,128)(2,1)S(1)}, u32[]{:S(2)}, u32[]{:S(2)}) %collective-permute-start.51) | collective-permute-done | bytes 294944 | tf_op jit(solution)/shard_map/ppermute | solution.py:243
  579.0 20.7 %collective-permute-done.43 = bf16[2,96,1024]{2,1,0:T(8,128)(2,1)S(1)} collective-permute-done((bf16[2,96,1024]{2,1,0:T(8,128)(2,1)S(1)}, bf16[2,96,1024]{2,1,0:T(8,128)(2,1)S(1)}, u32[]{:S(2)}, u32[]{:S(2)}) %collective-permute-start.43) | collective-permute-done | bytes 393248 | tf_op jit(solution)/shard_map/ppermute | solution.py:243
  672.9 11.4 %collective-permute-done.33 = bf16[384,1536]{1,0:T(8,128)(2,1)S(1)} collective-permute-done((bf16[384,1536]{1,0:T(8,128)(2,1)S(1)}, bf16[384,1536]{1,0:T(8,128)(2,1)S(1)}, u32[]{:S(2)}, u32[]{:S(2)}) %collective-permute-start.33) | collective-permute-done | bytes 1179680 | tf_op jit(solution)/shard_map/ppermute | solution.py:243
  690.9 16.6 %collective-permute-done.61 = bf16[2,192,1152]{2,1,0:T(8,128)(2,1)S(1)} collective-permute-done((bf16[2,192,1152]{2,1,0:T(8,128)(2,1)S(1)}, bf16[2,192,1152]{2,1,0:T(8,128)(2,1)S(1)}, u32[]{:S(2)}, u32[]{:S(2)}) %collective-permute-start.61) | collective-permute-done | bytes 884768 | tf_op jit(solution)/shard_map/ppermute | solution.py:243
  (447 shorter events, 313.8 us)
Async XLA Ops:
  7.2 241.4 %all-gather.5.cloned.1.call-start = ((), (), s32[]{:S(2)}) async-start(), calls=%async_computation.6 | async-start | bytes 8847360 | tf_op jit(solution)/shard_map/all_gather | solution.py:296
  23.6 46.4 %collective-permute-start.21 = (bf16[192,2304]{1,0:T(8,128)(2,1)}, bf16[192,2304]{1,0:T(8,128)(2,1)}, u32[]{:S(2)}, u32[]{:S(2)}) collective-permute-start(bf16[192,2304]{1,0:T(8,128)(2,1)} %pad_maximum_fusion.20), channel_id=1, source_target_pairs={{0,2},{1,3},{2,0},{3,1},{4,6},{5,7},{6,4},{7,5},{8,10},{9,11},{10,... | collective-permute-start | bytes 2654216 | tf_op jit(solution)/shard_map/ppermute | solution.py:243
  60.8 39.1 %collective-permute-start.4 = (bf16[2,2,96,1152]{3,2,1,0:T(8,128)(2,1)}, bf16[2,2,96,1152]{3,2,1,0:T(8,128)(2,1)}, u32[]{:S(2)}, u32[]{:S(2)}) collective-permute-start(bf16[2,2,96,1152]{3,2,1,0:T(8,128)(2,1)} %pad_maximum_fusion.16), channel_id=1, source_target_pairs={{0,16},{1,17},{2,18},{3,19},{4,20},{5,21},{6,22},{7,23},{8,24},{9,... | collective-permute-start | bytes 2654216 | tf_op jit(solution)/shard_map/ppermute | solution.py:243
  62.3 42.9 %collective-permute-start.6 = (bf16[2,2,96,1152]{3,2,1,0:T(8,128)(2,1)}, bf16[2,2,96,1152]{3,2,1,0:T(8,128)(2,1)}, u32[]{:S(2)}, u32[]{:S(2)}) collective-permute-start(bf16[2,2,96,1152]{3,2,1,0:T(8,128)(2,1)} %pad_maximum_fusion.17), channel_id=1, source_target_pairs={{0,2},{1,3},{2,0},{3,1},{4,6},{5,7},{6,4},{7,5},{8,10},{9,11},{10,... | collective-permute-start | bytes 2654216 | tf_op jit(solution)/shard_map/ppermute | solution.py:243
  72.9 230.1 %all-gather.7.cloned.1.call-start = ((), (), s32[]{:S(2)}) async-start(), calls=%async_computation.7 | async-start | bytes 4423680 | tf_op jit(solution)/shard_map/all_gather | solution.py:296
  91.8 49.7 %collective-permute-start.15 = (bf16[192,1152]{1,0:T(8,128)(2,1)}, bf16[192,1152]{1,0:T(8,128)(2,1)}, u32[]{:S(2)}, u32[]{:S(2)}) collective-permute-start(bf16[192,1152]{1,0:T(8,128)(2,1)} %select_select_fusion.4), channel_id=1, source_target_pairs={{0,2},{1,3},{2,0},{3,1},{4,6},{5,7},{6,4},{7,5},{8,10},{9,11},{10,... | collective-permute-start | bytes 1327112 | tf_op jit(solution)/shard_map/ppermute | solution.py:243
  97.7 36.0 %collective-permute-start.13 = (bf16[2,2,96,768]{3,2,1,0:T(8,128)(2,1)}, bf16[2,2,96,768]{3,2,1,0:T(8,128)(2,1)}, u32[]{:S(2)}, u32[]{:S(2)}) collective-permute-start(bf16[2,2,96,768]{3,2,1,0:T(8,128)(2,1)} %pad_maximum_fusion.25), channel_id=1, source_target_pairs={{0,2},{1,3},{2,0},{3,1},{4,6},{5,7},{6,4},{7,5},{8,10},{9,11},{10,... | collective-permute-start | bytes 1769480 | tf_op jit(solution)/shard_map/ppermute | solution.py:243
  167.6 40.3 %collective-permute-start.17 = (bf16[2,384,1536]{2,1,0:T(8,128)(2,1)}, bf16[2,384,1536]{2,1,0:T(8,128)(2,1)}, u32[]{:S(2)}, u32[]{:S(2)}) collective-permute-start(bf16[2,384,1536]{2,1,0:T(8,128)(2,1)} %pad_maximum_fusion), channel_id=1, source_target_pairs={{0,16},{1,3},{2,18},{3,1},{4,20},{5,7},{6,22},{7,5},{8,24},{9,11},... | collective-permute-start | bytes 7077896 | tf_op jit(solution)/shard_map/ppermute | solution.py:243
  170.9 68.1 %collective-permute-start.24 = (bf16[384,1536]{1,0:T(8,128)(2,1)S(1)}, bf16[384,1536]{1,0:T(8,128)(2,1)}, u32[]{:S(2)}, u32[]{:S(2)}) collective-permute-start(bf16[384,1536]{1,0:T(8,128)(2,1)S(1)} %bitcast.405), channel_id=1, source_target_pairs={{0,1},{1,0},{2,3},{3,2},{4,5},{5,4},{6,7},{7,6},{8,9},{9,8},{10,11... | collective-permute-start | bytes 3538952 | tf_op jit(solution)/shard_map/ppermute | solution.py:243
  170.9 324.8 %reduce-scatter.8.cloned.1.call-start = ((), (), s32[]{:S(2)}) async-start(), calls=%async_computation.5 | async-start | bytes 4423680 | tf_op jit(solution)/shard_map/reduce_scatter | solution.py:301
  210.3 32.1 %collective-permute-start.20 = (bf16[2,384,1536]{2,1,0:T(8,128)(2,1)}, bf16[2,384,1536]{2,1,0:T(8,128)(2,1)S(1)}, u32[]{:S(2)}, u32[]{:S(2)}) collective-permute-start(bf16[2,384,1536]{2,1,0:T(8,128)(2,1)} %collective-permute-done.17), channel_id=1, source_target_pairs={{0,1},{1,0},{2,3},{3,2},{4,5},{5,4},{6,7},{7,6},{8,9},{9,8},{10,11... | collective-permute-start | bytes 7077896 | tf_op jit(solution)/shard_map/ppermute | solution.py:243
  350.1 299.6 %reduce-scatter.4.cloned.1.call-start = ((), (), s32[]{:S(2)}) async-start(), calls=%async_computation.3 | async-start | bytes 4423680 | tf_op jit(solution)/shard_map/reduce_scatter | solution.py:301
  376.3 39.5 %collective-permute-start.29 = (bf16[2,384,1536]{2,1,0:T(8,128)(2,1)S(1)}, bf16[2,384,1536]{2,1,0:T(8,128)(2,1)}, u32[]{:S(2)}, u32[]{:S(2)}) collective-permute-start(bf16[2,384,1536]{2,1,0:T(8,128)(2,1)S(1)} %bitcast.421), channel_id=1, source_target_pairs={{0,16},{1,3},{2,18},{3,1},{4,20},{5,7},{6,22},{7,5},{8,24},{9,11},... | collective-permute-start | bytes 7077896 | tf_op jit(solution)/shard_map/ppermute | solution.py:243
  397.4 254.8 %reduce-scatter.6.cloned.1.call-start = ((), (), s32[]{:S(2)}) async-start(), calls=%async_computation.4 | async-start | bytes 4423680 | tf_op jit(solution)/shard_map/reduce_scatter | solution.py:301
  429.5 48.2 %collective-permute-start.27 = (bf16[1536,1536]{1,0:T(8,128)(2,1)}, bf16[1536,1536]{1,0:T(8,128)(2,1)}, u32[]{:S(2)}, u32[]{:S(2)}) collective-permute-start(bf16[1536,1536]{1,0:T(8,128)(2,1)} %convolution_convert_fusion.2), channel_id=1, source_target_pairs={{0,1},{1,0},{2,3},{3,2},{4,5},{5,4},{6,7},{7,6},{8,9},{9,8},{10,11... | collective-permute-start | bytes 14155784 | tf_op jit(solution)/shard_map/ppermute | solution.py:243
  502.1 73.5 %collective-permute-start.35 = (bf16[384,1536]{1,0:T(8,128)(2,1)}, bf16[384,1536]{1,0:T(8,128)(2,1)S(1)}, u32[]{:S(2)}, u32[]{:S(2)}) collective-permute-start(bf16[384,1536]{1,0:T(8,128)(2,1)} %fusion.39), channel_id=1, source_target_pairs={{0,1},{1,0},{2,3},{3,2},{4,5},{5,4},{6,7},{7,6},{8,9},{9,8},{10,11... | collective-permute-start | bytes 3538952 | tf_op jit(solution)/shard_map/ppermute | solution.py:243
  502.8 36.7 %collective-permute-start.42 = (bf16[2,2,96,1024]{3,2,0,1:T(8,128)(2,1)S(1)}, bf16[2,2,96,1024]{3,2,0,1:T(8,128)(2,1)S(1)}, u32[]{:S(2)}, u32[]{:S(2)}) collective-permute-start(bf16[2,2,96,1024]{3,2,0,1:T(8,128)(2,1)S(1)} %bitcast.431), channel_id=1, source_target_pairs={{0,2},{1,3},{2,0},{3,1},{4,6},{5,7},{6,4},{7,5},{8,10},{9,11},{10,... | collective-permute-start | bytes 2359304 | tf_op jit(solution)/shard_map/ppermute | solution.py:243
  510.0 30.6 %collective-permute-start.44 = (bf16[2,2,96,1024]{3,2,0,1:T(8,128)(2,1)S(1)}, bf16[2,2,96,1024]{3,2,0,1:T(8,128)(2,1)S(1)}, u32[]{:S(2)}, u32[]{:S(2)}) collective-permute-start(bf16[2,2,96,1024]{3,2,0,1:T(8,128)(2,1)S(1)} %bitcast.430), channel_id=1, source_target_pairs={{0,16},{1,17},{2,18},{3,19},{4,20},{5,21},{6,22},{7,23},{8,24},{9,... | collective-permute-start | bytes 2359304 | tf_op jit(solution)/shard_map/ppermute | solution.py:243
  522.7 131.9 %collective-permute-start.32 = (bf16[2,384,1536]{2,1,0:T(8,128)(2,1)}, bf16[2,384,1536]{2,1,0:T(8,128)(2,1)}, u32[]{:S(2)}, u32[]{:S(2)}) collective-permute-start(bf16[2,384,1536]{2,1,0:T(8,128)(2,1)} %bitcast.73), channel_id=1, source_target_pairs={{0,16},{1,3},{2,18},{3,1},{4,20},{5,7},{6,22},{7,5},{8,24},{9,11},... | collective-permute-start | bytes 7077896 | tf_op jit(solution)/shard_map/ppermute | solution.py:243
  523.6 41.0 %collective-permute-start.51 = (bf16[2,96,768]{2,1,0:T(8,128)(2,1)S(1)}, bf16[2,96,768]{2,1,0:T(8,128)(2,1)S(1)}, u32[]{:S(2)}, u32[]{:S(2)}) collective-permute-start(bf16[2,96,768]{2,1,0:T(8,128)(2,1)S(1)} %dynamic-slice_bitcast_fusion.6), channel_id=1, source_target_pairs={{0,16},{1,17},{2,18},{3,19},{4,20},{5,21},{6,22},{7,23},{8,24},{9,... | collective-permute-start | bytes 884744 | tf_op jit(solution)/shard_map/ppermute | solution.py:243
  572.2 56.8 %collective-permute-start.63 = (bf16[2,192,1152]{2,1,0:T(8,128)(2,1)}, bf16[2,192,1152]{2,1,0:T(8,128)(2,1)}, u32[]{:S(2)}, u32[]{:S(2)}) collective-permute-start(bf16[2,192,1152]{2,1,0:T(8,128)(2,1)} %pad_maximum_fusion.23), channel_id=1, source_target_pairs={{0,16},{1,17},{2,18},{3,19},{4,20},{5,21},{6,22},{7,23},{8,24},{9,... | collective-permute-start | bytes 2654216 | tf_op jit(solution)/shard_map/ppermute | solution.py:243
  575.6 34.0 %collective-permute-start.57 = (bf16[96,768]{1,0:T(8,128)(2,1)S(1)}, bf16[96,768]{1,0:T(8,128)(2,1)S(1)}, u32[]{:S(2)}, u32[]{:S(2)}) collective-permute-start(bf16[96,768]{1,0:T(8,128)(2,1)S(1)} %fusion.78), channel_id=1, source_target_pairs={{0,16},{1,17},{2,18},{3,19},{4,20},{5,21},{6,22},{7,23},{8,24},{9,... | collective-permute-start | bytes 442376 | tf_op jit(solution)/shard_map/ppermute | solution.py:243
  600.6 58.8 %collective-permute-start.36 = (bf16[384,1536]{1,0:T(8,128)(2,1)S(1)}, bf16[384,1536]{1,0:T(8,128)(2,1)}, u32[]{:S(2)}, u32[]{:S(2)}) collective-permute-start(bf16[384,1536]{1,0:T(8,128)(2,1)S(1)} %add_convert_fusion.2), channel_id=1, source_target_pairs={{0,1},{1,0},{2,3},{3,2},{4,5},{5,4},{6,7},{7,6},{8,9},{9,8},{10,11... | collective-permute-start | bytes 3538952 | tf_op jit(solution)/shard_map/ppermute | solution.py:243
  671.9 35.7 %collective-permute-start.61 = (bf16[2,192,1152]{2,1,0:T(8,128)(2,1)S(1)}, bf16[2,192,1152]{2,1,0:T(8,128)(2,1)S(1)}, u32[]{:S(2)}, u32[]{:S(2)}) collective-permute-start(bf16[2,192,1152]{2,1,0:T(8,128)(2,1)S(1)} %pad_maximum_fusion.22), channel_id=1, source_target_pairs={{0,16},{1,17},{2,18},{3,19},{4,20},{5,21},{6,22},{7,23},{8,24},{9,... | collective-permute-start | bytes 2654216 | tf_op jit(solution)/shard_map/ppermute | solution.py:243
  (111 other events, 1619.9 us)
Sparse Core Ops, SparseCore 0:
  73.0 125.4 all-gather.4
  200.0 68.0 all-gather.6
  350.2 62.8 reduce-scatter.7
  415.3 66.6 reduce-scatter.3
  484.1 66.6 reduce-scatter.5
